TPU v7x, 256 devices: a whole 4x4x8 slice. The times are simulated.
256 devices in a mesh: inp: 32 (over y, z_hi, core), tm: 8 (over z_lo, x).
Axes of the slice: x: 4, y: 4, z: 8 (z_hi: 4, z_lo: 2; z = z_hi * 2 + z_lo), core: 2. Of those that a mesh axis runs over, the one named last changes fastest.
Arguments:
- voltages: bfloat16 [512, 524288], P('inp', 'tm'), may hold values from -6 to 6
- taps: float32 [4, 512], replicated, may hold values from -3 to 3
Outputs:
- visibility: float32 [256, 2, 512, 512], P(('inp', 'tm'))
All inputs are finite; a program needn't handle non-finite values.
Results may differ from a plain program's by a relative error of at most 0.0038.
Values may be sent and summed in bfloat16 or wider, within the bound.
A program may use at most 128 MiB of HBM per device.

v0:
```python
import math

import jax
import jax.numpy as jnp
from jax import lax
from jax.sharding import PartitionSpec as P


def from_behind(block, axis, distance):
    devices = range(lax.axis_size(axis))
    route = [(i - distance, i) for i in devices if i - distance in devices]
    return lax.ppermute(block, axis, route)


def grouped_table(width, per_device):
    sample_idx = lax.broadcasted_iota(jnp.int32, (width, width), 0)
    column = lax.broadcasted_iota(jnp.int32, (width, width), 1)
    group = column // (2 * per_device)
    plane = column % (2 * per_device) // per_device
    channel = group * per_device + column % per_device
    phase = sample_idx * channel % width
    angle = phase.astype(jnp.float32) * (2.0 * math.pi / width)
    cosine = jnp.cos(angle).astype(jnp.bfloat16)
    sine = (-jnp.sin(angle)).astype(jnp.bfloat16)
    return jnp.where(plane == 0, cosine, sine)


def correlate(real_part, imag_part, scale):
    stacked = jnp.concatenate([real_part, imag_part], axis=2)
    rotated = jnp.concatenate([imag_part, -real_part], axis=2)
    cross_real = jnp.einsum("rcs,qcs->crq", stacked, stacked, preferred_element_type=jnp.float32)
    cross_imag = jnp.einsum("rcs,qcs->crq", rotated, stacked, preferred_element_type=jnp.float32)
    return jnp.stack([cross_real, cross_imag], axis=1) * scale


def local(voltages, taps):
    inp_dev = voltages.shape[0]
    tap_count = taps.shape[0]
    width = taps.shape[1]
    spectra_count = voltages.shape[1] // width
    time_devices = lax.axis_size("tm")
    per_device = width // 2 // (lax.axis_size("inp") * time_devices)
    inputs_all = inp_dev * lax.axis_size("inp")
    scale = 1.0 / (spectra_count * time_devices * width)
    sample_blocks = voltages.reshape(inp_dev, spectra_count, width)
    history = from_behind(sample_blocks[:, spectra_count - (tap_count - 1) :, :], "tm", 1)
    padded = jnp.concatenate([history, sample_blocks], axis=1)
    filtered = jnp.zeros((inp_dev, spectra_count, width), jnp.float32)
    for tap in range(tap_count):
        filtered = filtered + taps[tap][None, None, :] * padded[
            :, tap : tap + spectra_count, :
        ].astype(jnp.float32)
    filtered = filtered.astype(jnp.bfloat16)
    table = grouped_table(width, per_device)
    spectra = jnp.einsum("isn,nj->ijs", filtered, table, preferred_element_type=jnp.float32).astype(
        jnp.bfloat16
    )
    turned = lax.all_to_all(
        lax.all_to_all(spectra, "inp", split_axis=1, concat_axis=0, tiled=True),
        "tm",
        split_axis=1,
        concat_axis=2,
        tiled=True,
    )
    planes = turned.reshape(inputs_all, 2, per_device, turned.shape[2])
    return correlate(planes[:, 0], planes[:, 1], scale)


def solution(mesh):
    in_specs = (P("inp", "tm"), P())
    out_specs = P(("inp", "tm"), None, None, None)
    return jax.shard_map(local, mesh=mesh, in_specs=in_specs, out_specs=out_specs, check_vma=False)
```

profile of v0, /device:TPU:1, one launch (start us, length us, event | category | flops | bytes accessed | tf_op | source)
XLA Modules:
  0.0 123.3 jit_solution(15991717198502754298)
XLA Ops:
  0.0 0.0 copy-start.2
  0.0 2.3 %copy.23 = bf16[2,8,128,512]{3,2,1,0:T(8,128)(2,1)S(1)} copy(bf16[2,8,128,512]{3,1,2,0:T(8,128)(2,1)} %bitcast.45) | data formatting | bytes 4194304
  2.3 3.9 %collective-permute-start = (bf16[16,3,512]{2,1,0:T(4,128)(2,1)S(1)}, bf16[16,3,512]{2,1,0:T(4,128)(2,1)S(1)}, u32[]{:S(2)}, u32[]{:S(2)}) collective-permute-start(bf16[16,3,512]{2,1,0:T(4,128)(2,1)S(1)} %slice.40), channel_id=1, source_target_pairs={{0,1},{1,2},{2,3},{3,4},{4,5},{5,6},{6,7},{8,9},{9,10},{10,11},{11... | collective-permute-start | bytes 147464 | tf_op jit(solution)/shard_map/ppermute | solution.py:12
  6.3 0.0 copy-done.2
  6.4 1.2 %collective-permute-done = bf16[16,3,512]{2,1,0:T(4,128)(2,1)S(1)} collective-permute-done((bf16[16,3,512]{2,1,0:T(4,128)(2,1)S(1)}, bf16[16,3,512]{2,1,0:T(4,128)(2,1)S(1)}, u32[]{:S(2)}, u32[]{:S(2)}) %collective-permute-start) | collective-permute-done | bytes 49184 | tf_op jit(solution)/shard_map/ppermute | solution.py:12
  7.6 7.0 %convert_bitcast_fusion = bf16[16,512,128]{2,1,0:T(8,128)(2,1)S(1)} fusion(bf16[16,128,512]{2,1,0:T(8,128)(2,1)S(1)} %bitcast.44, bf16[16,3,512]{2,1,0:T(4,128)(2,1)S(1)} %collective-permute-done, f32[512]{0:T(512)S(1)} %bitcast.48, f32[512]{0:T(512)S(1)} %bitcast.49, f32[512]{0:T(512)S(1)} %bitcast.47, f32[512]{0:T(512)S(1)} %bitcast.46, ...), kind=kOutput, calls=%fused_computation.12 | convolution fusion | flops 1102315520 | bytes 4260864 | tf_op jit(solution)/shard_map/isn,nj->ijs/dot_general | solution.py:55
  14.6 1.4 %copy.14 = bf16[16,512,128]{2,0,1:T(8,128)(2,1)S(1)} copy(bf16[16,512,128]{2,1,0:T(8,128)(2,1)S(1)} %convert_bitcast_fusion) | data formatting | bytes 4194304 | tf_op jit(solution)/shard_map/convert_element_type | solution.py:55
  16.0 54.6 %all_to_all.33 = bf16[16,512,128]{2,0,1:T(8,128)(2,1)S(1)} all-to-all(bf16[16,512,128]{2,0,1:T(8,128)(2,1)S(1)} %copy.14), channel_id=1, replica_groups=mesh['inp'=32,'tm'=8] {'inp'}, dimensions={1} | all-to-all | bytes 4194304 | tf_op jit(solution)/shard_map/all_to_all | solution.py:59
  70.5 0.5 copy.16
  71.1 0.5 copy.17
  71.6 40.8 %all_to_all.34 = bf16[512,16,128]{2,0,1:T(8,128)(2,1)} all-to-all(bf16[512,16,128]{2,0,1:T(8,128)(2,1)S(1)} %copy.17), channel_id=1, replica_groups=mesh['inp'=32,'tm'=8] {'tm'}, dimensions={1} | all-to-all | bytes 4194304 | tf_op jit(solution)/shard_map/all_to_all | solution.py:58
  112.4 2.9 %copy.18 = bf16[512,2,8,128]{0,3,2,1:T(8,128)(2,1)S(1)} copy(bf16[512,2,8,128]{3,0,1,2:T(8,128)(2,1)} %bitcast.41) | data formatting | bytes 4194304 | tf_op jit(solution)/shard_map/all_to_all | solution.py:58
  115.3 1.0 fusion.36
  116.3 1.1 slice_bitcast_fusion
  117.4 0.5 copy.19
  117.9 0.0 copy-start.1
  118.0 0.5 copy.20
  118.5 0.7 copy-done.1
  119.2 0.0 copy-start
  119.2 1.3 %convolution_bitcast_fusion = f32[1,1,512,512]{3,2,1,0:T(8,128)S(1)} fusion(bf16[512,1,1024]{0,2,1:T(8,128)(2,1)S(1)} %copy.20, bf16[512,1,1024]{0,2,1:T(8,128)(2,1)S(1)} %copy-done.1), kind=kOutput, calls=%fused_computation.18 | convolution fusion | flops 1077936128 | bytes 3145728 | tf_op jit(solution)/shard_map/rcs,qcs->crq/dot_general | solution.py:31
  120.4 0.0 copy-done
  120.5 1.3 %fusion.6 = f32[1,1,512,512]{3,2,1,0:T(8,128)S(1)} fusion(bf16[512,1,1024]{0,2,1:T(8,128)(2,1)S(1)} %copy-done, bf16[512,1,1024]{0,2,1:T(8,128)(2,1)S(1)} %copy.20, bf16[512,1,1024]{0,2,1:T(8,128)(2,1)S(1)} %copy-done.1), kind=kOutput, calls=%fused_computation.17 | convolution fusion | flops 1082130432 | bytes 4194304 | tf_op jit(solution)/shard_map/rcs,qcs->crq/dot_general | solution.py:32
  121.7 1.6 %maximum_multiply_fusion = f32[1,2,512,512]{3,2,1,0:T(8,128)} fusion(f32[1,1,512,512]{3,2,1,0:T(8,128)S(1)} %fusion.6, f32[1,1,512,512]{3,2,1,0:T(8,128)S(1)} %convolution_bitcast_fusion), kind=kLoop, calls=%fused_computation.11 | loop fusion | flops 1048576 | bytes 4194304 | tf_op jit(solution)/shard_map/mul | solution.py:33
  (5 shorter events, 0.1 us)
Async XLA Ops:
  0.0 6.3 %copy-start.2 = (f32[4,512]{1,0:T(4,128)S(1)}, f32[4,512]{1,0:T(4,128)}, u32[]{:S(2)}) copy-start(f32[4,512]{1,0:T(4,128)} %param.3) | copy-start | bytes 24580
  2.3 5.3 %collective-permute-start = (bf16[16,3,512]{2,1,0:T(4,128)(2,1)S(1)}, bf16[16,3,512]{2,1,0:T(4,128)(2,1)S(1)}, u32[]{:S(2)}, u32[]{:S(2)}) collective-permute-start(bf16[16,3,512]{2,1,0:T(4,128)(2,1)S(1)} %slice.40), channel_id=1, source_target_pairs={{0,1},{1,2},{2,3},{3,4},{4,5},{5,6},{6,7},{8,9},{9,10},{10,11},{11... | collective-permute-start | bytes 147464 | tf_op jit(solution)/shard_map/ppermute | solution.py:12
  117.9 1.2 copy-start.1
  119.2 1.3 %copy-start = (bf16[512,1,1024]{0,2,1:T(8,128)(2,1)S(1)}, bf16[512,1,1024]{0,2,1:T(8,128)(2,1)}, u32[]{:S(2)}) copy-start(bf16[512,1,1024]{0,2,1:T(8,128)(2,1)} %fusion.36) | copy-start | bytes 3145732
where the time goes:
time: 124 us; the launch traced here: 123 us
  blocking collectives  95.4 us (77%)
  local copies, waits for them, and re-layouts  10.5 us (8%)
  matrix products  9.53 us (8%)
  starting transfers between devices  3.95 us (3%)
  other arithmetic  2.61 us (2%)
  waiting for transfers between devices  1.25 us (1%)
    all_to_all x1, blocking collectives, local(): lax.all_to_all(spectra, 'inp', split_axis=1, concat_axis=0, tiled=True)  54.6 us
    all_to_all x1, blocking collectives, local(): lax.all_to_all(lax.all_to_all(spectra, 'inp', split_axis=1, concat_axis=0...  40.8 us
    dot_general x1, matrix products, local(): jnp.einsum('isn,nj->ijs', filtered, table, preferred_element_type=jnp.flo...  6.98 us
    ppermute x1, starting transfers between devices, from_behind(): return lax.ppermute(block, axis, route)  3.95 us
    unnamed x7, local copies, waits for them, and re-layouts  2.96 us
    all_to_all x1, local copies, waits for them, and re-layouts, local(): lax.all_to_all(lax.all_to_all(spectra, 'inp', split_axis=1, concat_axis=0...  2.85 us
  transfers between devices with their start and end apart: 1, of which 1 were waited for; matrix products, arithmetic and copies ran while one was open for 0% of the time, Pallas kernels for 0%

commit v1 on v0

v1 whole, which is shorter than its diff:
```python
import functools
import math

import jax
import jax.numpy as jnp
import ml_dtypes
import numpy as np
from jax import lax
from jax.experimental import pallas as pl
from jax.experimental.pallas import tpu as pltpu
from jax.sharding import PartitionSpec as P

MESH = pl.DeviceIdType.MESH
NX, NY, NZ, NC, ZL = 4, 4, 8, 2, 2
ZH = NZ // ZL
PLANE = NY * NX * NC
HALF = 8
LANES = 128


def position():
    inp = lax.axis_index("inp")
    tm = lax.axis_index("tm")
    return tm % NX, inp // (ZH * NC), (inp // NC) % ZH * ZL + tm // NX, inp % NC


def device(x, y, z, c):
    return (y * ZH + z // ZL) * NC + c, (z % ZL) * NX + x


def channel_of_row():
    order = np.empty((NY, NX, NC, NZ), np.int64)
    for y in range(NY):
        for x in range(NX):
            for c in range(NC):
                for z in range(NZ):
                    inp, tm = device(x, y, z, c)
                    order[y, x, c, z] = inp * (ZL * NX) + tm
    return order.reshape(-1)


def dft_rows(width):
    channel = channel_of_row()
    phase = (channel[:, None] * np.arange(width)[None, :]) % width
    angle = phase.astype(np.float32) * np.float32(2.0 * math.pi / width)
    rows = np.concatenate([np.cos(angle), -np.sin(angle)], axis=0)
    return rows.astype(ml_dtypes.bfloat16)


def exchange_kernel(
    v_hbm, taps_ref, table_ref, r_ref,
    v, hist, f32s, s32, sa, sb, za, yb,
    load_sem, hist_send, hist_recv, local_sem,
    za_send, za_recv, xa_send, xa_recv, xb_send, xb_recv, zb_send, zb_recv,
):
    x, y, z, c = position()
    zh, zl = z // ZL, z % ZL
    tm = lax.axis_index("tm")
    inp = lax.axis_index("inp")
    tms = ZL * NX
    width = taps_ref.shape[1]
    spectra = v.shape[1] // width
    rows = v.shape[0]
    taps_n = taps_ref.shape[0]

    load = pltpu.make_async_copy(v_hbm, v, load_sem)
    load.start()

    def z_peer(dz):
        zz = (z + dz) % NZ
        return zz, device(x, y, zz, c)

    def plane_peer(i):
        xx = (x + i // (NY * NC)) % NX
        yy = (y + (i // NC) % NY) % NY
        cc = (c + i % NC) % NC
        return xx, yy, cc, device(xx, yy, z, cc)

    later = (inp, (tm + 1) % tms)
    earlier = (inp, (tm + tms - 1) % tms)
    barrier = pltpu.get_barrier_semaphore()
    pl.semaphore_signal(barrier, inc=1, device_id=later, device_id_type=MESH)
    pl.semaphore_signal(barrier, inc=1, device_id=earlier, device_id_type=MESH)
    for dz in range(1, NZ):
        pl.semaphore_signal(barrier, inc=1, device_id=z_peer(dz)[1], device_id_type=MESH)

    def greet(i, _):
        pl.semaphore_signal(barrier, inc=1, device_id=plane_peer(i)[3], device_id_type=MESH)
        return 0

    lax.fori_loop(1, PLANE, greet, 0)
    pl.semaphore_wait(barrier, 2 + NZ - 1 + PLANE - 1)

    history = pltpu.make_async_remote_copy(
        src_ref=v_hbm.at[:, pl.ds((spectra - (taps_n - 1)) * width, (taps_n - 1) * width)],
        dst_ref=hist,
        send_sem=hist_send,
        recv_sem=hist_recv,
        device_id=later,
        device_id_type=MESH,
    )
    history.start()
    load.wait()

    gains = [
        jnp.broadcast_to(taps_ref[t : t + 1, :], (rows, width)) for t in range(taps_n)
    ]

    def block(ref, s):
        return ref[:, pl.ds(pl.multiple_of(s * width, width), width)].astype(jnp.float32)

    def weigh(past):
        total = gains[0] * past[0]
        for t in range(1, taps_n):
            total = total + gains[t] * past[t]
        return total

    def put(s, value):
        for q in range(width // LANES):
            f32s.at[q][pl.ds(s, rows, stride=spectra), :] = value[:, q * LANES : (q + 1) * LANES]

    def step(s, past):
        past = past + (block(v, s),)
        put(s, weigh(past))
        return past[1:]

    first = tuple(block(v, s) for s in range(taps_n - 1))
    lax.fori_loop(taps_n - 1, spectra, step, first)

    history.wait()
    seen = tm > 0
    past = tuple(
        jnp.where(seen, block(hist, s), 0.0) for s in range(taps_n - 1)
    )
    for s in range(taps_n - 1):
        past = step(s, past)

    def transform(half, out):
        def pair(p, _):
            i = half * HALF + 2 * p
            at = pl.ds(pl.multiple_of(i * spectra, LANES), 2 * spectra)
            f = jnp.concatenate(
                [f32s[q, at, :] for q in range(width // LANES)], axis=1
            ).astype(jnp.bfloat16)
            spec = lax.dot_general(
                table_ref[...], f, (((1,), (1,)), ((), ())), preferred_element_type=jnp.float32
            )
            for two in range(2):
                for plane in range(2):
                    s32.at[plane][pl.ds(2 * p + two, width // 2, stride=HALF), :] = spec[
                        plane * (width // 2) : (plane + 1) * (width // 2),
                        two * spectra : (two + 1) * spectra,
                    ]
            return 0

        lax.fori_loop(0, HALF // 2, pair, 0)

        def pack(m, _):
            at = pl.ds(pl.multiple_of(m * NZ * HALF, NZ * HALF), NZ * HALF)
            both = jnp.concatenate([s32[0, at, :], s32[1, at, :]], axis=1)
            out[m] = both.reshape(NZ, HALF, 2 * spectra).astype(jnp.bfloat16)
            return 0

        lax.fori_loop(0, PLANE, pack, 0)

    here = (y * NX + x) * NC + c

    transform(0, sa)

    def za_copy(dz):
        zz, peer = z_peer(dz)
        return pltpu.make_async_remote_copy(
            src_ref=sa.at[:, zz],
            dst_ref=za.at[zl, zh],
            send_sem=za_send.at[dz - 1],
            recv_sem=za_recv.at[dz - 1],
            device_id=peer,
            device_id_type=MESH,
        )

    for dz in (4, 3, 5, 2, 6, 1, 7):
        za_copy(dz).start()
    keep_a = pltpu.make_async_copy(sa.at[:, z], za.at[zl, zh], local_sem.at[0])
    keep_a.start()

    transform(1, sb)

    def xb_copy(i):
        xx, yy, cc, peer = plane_peer(i)
        return pltpu.make_async_remote_copy(
            src_ref=sb.at[(yy * NX + xx) * NC + cc],
            dst_ref=yb.at[x, y, c],
            send_sem=xb_send.at[i - 1],
            recv_sem=xb_recv.at[i - 1],
            device_id=peer,
            device_id_type=MESH,
        )

    def xb_start(i, _):
        xb_copy(i).start()
        return 0

    lax.fori_loop(1, PLANE, xb_start, 0)
    keep_b = pltpu.make_async_copy(sb.at[here], yb.at[x, y, c], local_sem.at[1])
    keep_b.start()

    def xb_wait(i, _):
        xb_copy(i).wait()
        return 0

    lax.fori_loop(1, PLANE, xb_wait, 0)
    keep_b.wait()

    def zb_copy(dz):
        zz, peer = z_peer(dz)
        return pltpu.make_async_remote_copy(
            src_ref=yb.at[:, :, :, zz],
            dst_ref=r_ref.at[zl, :, :, zh, :, 1],
            send_sem=zb_send.at[dz - 1],
            recv_sem=zb_recv.at[dz - 1],
            device_id=peer,
            device_id_type=MESH,
        )

    for dz in (4, 3, 5, 2, 6, 1, 7):
        zb_copy(dz).start()
    last_b = pltpu.make_async_copy(
        yb.at[:, :, :, z], r_ref.at[zl, :, :, zh, :, 1], local_sem.at[2]
    )
    last_b.start()

    for dz in range(1, NZ):
        za_copy(dz).wait()
    keep_a.wait()

    def xa_copy(i):
        xx, yy, cc, peer = plane_peer(i)
        return pltpu.make_async_remote_copy(
            src_ref=za.at[:, :, (yy * NX + xx) * NC + cc],
            dst_ref=r_ref.at[:, x, y, :, c, 0],
            send_sem=xa_send.at[i - 1],
            recv_sem=xa_recv.at[i - 1],
            device_id=peer,
            device_id_type=MESH,
        )

    def xa_start(i, _):
        xa_copy(i).start()
        return 0

    lax.fori_loop(1, PLANE, xa_start, 0)
    last_a = pltpu.make_async_copy(
        za.at[:, :, here], r_ref.at[:, x, y, :, c, 0], local_sem.at[3]
    )
    last_a.start()

    def xa_wait(i, _):
        xa_copy(i).wait()
        return 0

    lax.fori_loop(1, PLANE, xa_wait, 0)
    last_a.wait()
    for dz in range(1, NZ):
        zb_copy(dz).wait()
    last_b.wait()


def exchange(voltages, taps, table):
    inp_dev, samples = voltages.shape
    width = taps.shape[1]
    spectra = samples // width
    block = (HALF, 2 * spectra)
    bf16 = jnp.bfloat16
    dma = pltpu.SemaphoreType.DMA
    return pl.pallas_call(
        exchange_kernel,
        name="exchange",
        out_shape=jax.ShapeDtypeStruct((ZL, NX, NY, ZH, NC, inp_dev // HALF) + block, bf16),
        in_specs=[
            pl.BlockSpec(memory_space=pl.ANY),
            pl.BlockSpec(memory_space=pltpu.VMEM),
            pl.BlockSpec(memory_space=pltpu.VMEM),
        ],
        out_specs=pl.BlockSpec(memory_space=pltpu.VMEM),
        scratch_shapes=[
            pltpu.VMEM((inp_dev, samples), bf16),
            pltpu.VMEM((inp_dev, (taps.shape[0] - 1) * width), bf16),
            pltpu.VMEM((width // LANES, inp_dev * spectra, LANES), jnp.float32),
            pltpu.VMEM((2, width // 2 * HALF, spectra), jnp.float32),
            pltpu.VMEM((PLANE, NZ) + block, bf16),
            pltpu.VMEM((PLANE, NZ) + block, bf16),
            pltpu.VMEM((ZL, ZH, PLANE) + block, bf16),
            pltpu.VMEM((NX, NY, NC, NZ) + block, bf16),
            dma(()), dma(()), dma(()), dma((4,)),
            dma((NZ - 1,)), dma((NZ - 1,)),
            dma((PLANE - 1,)), dma((PLANE - 1,)),
            dma((PLANE - 1,)), dma((PLANE - 1,)),
            dma((NZ - 1,)), dma((NZ - 1,)),
        ],
        compiler_params=pltpu.CompilerParams(
            collective_id=0, has_side_effects=True, vmem_limit_bytes=48 << 20
        ),
    )(voltages, taps, table)


def correlate_kernel(scale, r_ref, o_ref):
    m = pl.program_id(0)
    size = o_ref.shape[2]
    times = r_ref.shape[0]
    half = r_ref.shape[2] // 2
    real = jnp.zeros(o_ref.shape[2:], jnp.float32)
    imag = jnp.zeros(o_ref.shape[2:], jnp.float32)
    contract = (((1,), (1,)), ((), ()))
    at = pl.ds(pl.multiple_of(m * size, size), size)
    for t in range(times):
        mine = r_ref[t, at, :]
        turned = jnp.concatenate([mine[:, half:], -mine[:, :half]], axis=1)
        every = r_ref[t]
        real += lax.dot_general(mine, every, contract, preferred_element_type=jnp.float32)
        imag += lax.dot_general(turned, every, contract, preferred_element_type=jnp.float32)
    o_ref[0, 0] = real * scale
    o_ref[0, 1] = imag * scale


def correlate(spectra, scale, size=128):
    inputs = spectra.shape[1]
    return pl.pallas_call(
        functools.partial(correlate_kernel, scale),
        name="correlate",
        grid=(inputs // size,),
        out_shape=jax.ShapeDtypeStruct((1, 2, inputs, inputs), jnp.float32),
        in_specs=[pl.BlockSpec(memory_space=pltpu.VMEM)],
        out_specs=pl.BlockSpec((1, 2, size, inputs), lambda m: (0, 0, m, 0)),
        compiler_params=pltpu.CompilerParams(vmem_limit_bytes=32 << 20),
    )(spectra)


def local(voltages, taps):
    width = taps.shape[1]
    table = jnp.asarray(dft_rows(width))
    times = lax.axis_size("tm")
    spectra = voltages.shape[1] // width
    scale = 1.0 / (spectra * times * width)
    gathered = exchange(voltages, taps, table)
    return correlate(gathered.reshape(times, -1, 2 * spectra), scale)


def solution(mesh):
    in_specs = (P("inp", "tm"), P())
    out_specs = P(("inp", "tm"), None, None, None)
    return jax.shard_map(local, mesh=mesh, in_specs=in_specs, out_specs=out_specs, check_vma=False)
```

time: 124 us -> 77.2 us (0.62)
  blocking collectives: 95.4 us -> 0 us
  Pallas kernels: 0 us -> 73.7 us
  matrix products: 9.53 us -> 0 us
  local copies, waits for them, and re-layouts: 10.5 us -> 3.33 us
  starting transfers between devices: 3.95 us -> 0 us
  other arithmetic: 2.61 us -> 0 us
  waiting for transfers between devices: 1.25 us -> 0 us
    all_to_all x2 -> x0, blocking collectives: 95.4 us -> none  [the longest x1 54.6 us: local(): lax.all_to_all(spectra, 'inp', split_axis=1, concat_axis=0, tiled=True)]
    pallas_call x0 -> x2, Pallas kernels: none -> 73.7 us  [the longest x1 67 us: exchange(): pl.pallas_call(exchange_kernel, name='exchange', out_shape=jax.ShapeDtype...]
    dot_general x3 -> x0, matrix products: 9.53 us -> none  [the longest x1 6.98 us: local(): jnp.einsum('isn,nj->ijs', filtered, table, preferred_element_type=jnp.flo...]
    ppermute x1 -> x0, starting transfers between devices: 3.95 us -> none  [from_behind(): return lax.ppermute(block, axis, route)]
    all_to_all x3 -> x0, local copies, waits for them, and re-layouts: 3.94 us -> none  [the longest x1 2.85 us: local(): lax.all_to_all(lax.all_to_all(spectra, 'inp', split_axis=1, concat_axis=0...]
    squeeze x2 -> x0, local copies, waits for them, and re-layouts: 1.65 us -> none  [local(): return correlate(planes[:, 0], planes[:, 1], scale)]
    mul x1 -> x0, other arithmetic: 1.55 us -> none  [correlate(): return jnp.stack([cross_real, cross_imag], axis=1) * scale]
    convert_element_type x1 -> x0, local copies, waits for them, and re-layouts: 1.35 us -> none  [local(): jnp.einsum('isn,nj->ijs', filtered, table, preferred_element_type=jnp.flo...]
  transfers between devices with their start and end apart: 1 -> 0, of which waited for: 1 -> 0; matrix products, arithmetic and copies ran while one was open for 0% -> 0% of each run, Pallas kernels for 0% -> 0%
where the time goes in v1:
time: 77.2 us; the launch traced here: 77 us
  Pallas kernels  73.7 us (95%)
  local copies, waits for them, and re-layouts  3.33 us (4%)
    pallas_call x1, Pallas kernels, exchange(): pl.pallas_call(exchange_kernel, name='exchange', out_shape=jax.ShapeDtype...  67 us
    pallas_call x1, Pallas kernels, correlate(): pl.pallas_call(functools.partial(correlate_kernel, scale), name='correlat...  6.73 us
    unnamed x6, local copies, waits for them, and re-layouts  3.33 us

profile of v1, /device:TPU:1, one launch (start us, length us, event | category | flops | bytes accessed | tf_op | source)
XLA Modules:
  0.0 77.0 jit_solution(7784725349489390312)
XLA Ops:
  0.0 0.0 copy-start
  0.0 1.6 %copy-done = bf16[16,65536]{1,0:T(8,128)(2,1)S(1)} copy-done((bf16[16,65536]{1,0:T(8,128)(2,1)S(1)}, bf16[16,65536]{1,0:T(8,128)(2,1)}, u32[]{:S(2)}) %copy-start) | copy-done | bytes 2097176
  1.6 0.0 copy-start.1
  1.6 1.0 %copy-done.1 = bf16[512,512]{1,0:T(8,128)(2,1)S(1)} copy-done((bf16[512,512]{1,0:T(8,128)(2,1)S(1)}, bf16[512,512]{1,0:T(8,128)(2,1)}, u32[]{:S(2)}) %copy-start.1) | copy-done | bytes 524312
  2.6 0.0 copy-start.2
  2.6 0.7 copy-done.2
  3.3 67.0 %exchange.1 = bf16[2,4,4,4,2,2,8,256]{7,6,5,4,3,2,1,0:T(8,128)(2,1)S(1)} custom-call(bf16[16,65536]{1,0:T(8,128)(2,1)S(1)} %copy-done, f32[4,512]{1,0:T(4,128)S(1)} %copy-done.2, bf16[512,512]{1,0:T(8,128)(2,1)S(1)} %copy-done.1), custom_call_target="tpu_custom_call" | custom-call | tf_op jit(solution)/shard_map/exchange/pallas_call | solution.py:275
  70.3 6.7 %correlate.1 = f32[1,2,512,512]{3,2,1,0:T(8,128)} custom-call(bf16[8,512,256]{2,1,0:T(8,128)(2,1)S(1)} %bitcast.1), custom_call_target="tpu_custom_call" | custom-call | tf_op jit(solution)/shard_map/correlate/pallas_call | solution.py:327
Async XLA Ops:
  0.0 1.6 %copy-start = (bf16[16,65536]{1,0:T(8,128)(2,1)S(1)}, bf16[16,65536]{1,0:T(8,128)(2,1)}, u32[]{:S(2)}) copy-start(bf16[16,65536]{1,0:T(8,128)(2,1)} %v_hbm.1) | copy-start | bytes 6291460
  1.6 1.0 %copy-start.1 = (bf16[512,512]{1,0:T(8,128)(2,1)S(1)}, bf16[512,512]{1,0:T(8,128)(2,1)}, u32[]{:S(2)}) copy-start(bf16[512,512]{1,0:T(8,128)(2,1)} %constant.2.clone.table_ref) | copy-start | bytes 1572868
  2.6 0.7 copy-start.2

commit v2 on v1

--- a/solution.py
+++ b/solution.py
@@ -16,6 +16,8 @@
 PLANE = NY * NX * NC
 HALF = 8
 LANES = 128
+PIECES = 4
+PITCH = 136
 
 
 def position():
@@ -48,8 +50,8 @@
 
 
 def exchange_kernel(
-    v_hbm, taps_ref, table_ref, r_ref,
-    v, hist, f32s, s32, sa, sb, za, yb,
+    v_hbm, taps_hbm, table_hbm, r_ref,
+    v, taps_ref, table_ref, hist, f32s, s32, sa, sb, za, yb,
     load_sem, hist_send, hist_recv, local_sem,
     za_send, za_recv, xa_send, xa_recv, xb_send, xb_recv, zb_send, zb_recv,
 ):
@@ -58,13 +60,21 @@
     tm = lax.axis_index("tm")
     inp = lax.axis_index("inp")
     tms = ZL * NX
-    width = taps_ref.shape[1]
+    taps_n, width = taps_ref.shape
     spectra = v.shape[1] // width
     rows = v.shape[0]
-    taps_n = taps_ref.shape[0]
-
-    load = pltpu.make_async_copy(v_hbm, v, load_sem)
-    load.start()
+    piece = spectra // PIECES
+
+    def load(g):
+        at = pl.ds(pl.multiple_of(g * piece * width, width), piece * width)
+        return pltpu.make_async_copy(v_hbm.at[:, at], v.at[:, at], load_sem.at[g])
+
+    load_taps = pltpu.make_async_copy(taps_hbm, taps_ref, load_sem.at[PIECES])
+    load_table = pltpu.make_async_copy(table_hbm, table_ref, load_sem.at[PIECES + 1])
+    load_taps.start()
+    for g in range(PIECES):
+        load(g).start()
+    load_table.start()
 
     def z_peer(dz):
         zz = (z + dz) % NZ
@@ -100,48 +110,58 @@
         device_id_type=MESH,
     )
     history.start()
-    load.wait()
-
-    gains = [
-        jnp.broadcast_to(taps_ref[t : t + 1, :], (rows, width)) for t in range(taps_n)
-    ]
-
-    def block(ref, s):
-        return ref[:, pl.ds(pl.multiple_of(s * width, width), width)].astype(jnp.float32)
-
-    def weigh(past):
+    load_taps.wait()
+
+    def block(ref, s, q):
+        at = pl.multiple_of(s * width + q * LANES, LANES)
+        return ref[:, pl.ds(at, LANES)].astype(jnp.float32)
+
+    def gain(q):
+        return [
+            jnp.broadcast_to(taps_ref[t : t + 1, q * LANES : (q + 1) * LANES], (rows, LANES))
+            for t in range(taps_n)
+        ]
+
+    def step(gains, s, q, past):
+        past = past + (block(v, s, q),)
         total = gains[0] * past[0]
         for t in range(1, taps_n):
             total = total + gains[t] * past[t]
-        return total
-
-    def put(s, value):
+        f32s.at[q][pl.ds(s, rows, stride=PITCH), :] = total
+        return past[1:]
+
+    def filter_piece(g, _):
+        load(g).wait()
         for q in range(width // LANES):
-            f32s.at[q][pl.ds(s, rows, stride=spectra), :] = value[:, q * LANES : (q + 1) * LANES]
-
-    def step(s, past):
-        past = past + (block(v, s),)
-        put(s, weigh(past))
-        return past[1:]
-
-    first = tuple(block(v, s) for s in range(taps_n - 1))
-    lax.fori_loop(taps_n - 1, spectra, step, first)
+            gains = gain(q)
+            past = tuple(
+                block(v, jnp.maximum(g * piece - k, 0), q) for k in range(taps_n - 1, 0, -1)
+            )
+            for j in range(piece):
+                past = step(gains, g * piece + j, q, past)
+        return 0
+
+    lax.fori_loop(0, PIECES, filter_piece, 0)
 
     history.wait()
     seen = tm > 0
-    past = tuple(
-        jnp.where(seen, block(hist, s), 0.0) for s in range(taps_n - 1)
-    )
-    for s in range(taps_n - 1):
-        past = step(s, past)
+    for q in range(width // LANES):
+        gains = gain(q)
+        past = tuple(jnp.where(seen, block(hist, s, q), 0.0) for s in range(taps_n - 1))
+        for s in range(taps_n - 1):
+            past = step(gains, s, q, past)
+    load_table.wait()
 
     def transform(half, out):
-        def pair(p, _):
+        def filtered(i):
+            return jnp.concatenate(
+                [f32s[q, i * PITCH : i * PITCH + spectra, :] for q in range(width // LANES)],
+                axis=1,
+            ).astype(jnp.bfloat16)
+
+        for p in range(HALF // 2):
             i = half * HALF + 2 * p
-            at = pl.ds(pl.multiple_of(i * spectra, LANES), 2 * spectra)
-            f = jnp.concatenate(
-                [f32s[q, at, :] for q in range(width // LANES)], axis=1
-            ).astype(jnp.bfloat16)
+            f = jnp.concatenate([filtered(i), filtered(i + 1)], axis=0)
             spec = lax.dot_general(
                 table_ref[...], f, (((1,), (1,)), ((), ())), preferred_element_type=jnp.float32
             )
@@ -151,9 +171,6 @@
                         plane * (width // 2) : (plane + 1) * (width // 2),
                         two * spectra : (two + 1) * spectra,
                     ]
-            return 0
-
-        lax.fori_loop(0, HALF // 2, pair, 0)
 
         def pack(m, _):
             at = pl.ds(pl.multiple_of(m * NZ * HALF, NZ * HALF), NZ * HALF)
@@ -272,26 +289,27 @@
     block = (HALF, 2 * spectra)
     bf16 = jnp.bfloat16
     dma = pltpu.SemaphoreType.DMA
+    operands = [
+        pltpu.with_memory_space_constraint(a, pltpu.HBM) for a in (voltages, taps, table)
+    ]
     return pl.pallas_call(
         exchange_kernel,
         name="exchange",
         out_shape=jax.ShapeDtypeStruct((ZL, NX, NY, ZH, NC, inp_dev // HALF) + block, bf16),
-        in_specs=[
-            pl.BlockSpec(memory_space=pl.ANY),
-            pl.BlockSpec(memory_space=pltpu.VMEM),
-            pl.BlockSpec(memory_space=pltpu.VMEM),
-        ],
+        in_specs=[pl.BlockSpec(memory_space=pltpu.HBM)] * 3,
         out_specs=pl.BlockSpec(memory_space=pltpu.VMEM),
         scratch_shapes=[
             pltpu.VMEM((inp_dev, samples), bf16),
+            pltpu.VMEM(taps.shape, taps.dtype),
+            pltpu.VMEM(table.shape, table.dtype),
             pltpu.VMEM((inp_dev, (taps.shape[0] - 1) * width), bf16),
-            pltpu.VMEM((width // LANES, inp_dev * spectra, LANES), jnp.float32),
+            pltpu.VMEM((width // LANES, inp_dev * PITCH, LANES), jnp.float32),
             pltpu.VMEM((2, width // 2 * HALF, spectra), jnp.float32),
             pltpu.VMEM((PLANE, NZ) + block, bf16),
             pltpu.VMEM((PLANE, NZ) + block, bf16),
             pltpu.VMEM((ZL, ZH, PLANE) + block, bf16),
             pltpu.VMEM((NX, NY, NC, NZ) + block, bf16),
-            dma(()), dma(()), dma(()), dma((4,)),
+            dma((PIECES + 2,)), dma(()), dma(()), dma((4,)),
             dma((NZ - 1,)), dma((NZ - 1,)),
             dma((PLANE - 1,)), dma((PLANE - 1,)),
             dma((PLANE - 1,)), dma((PLANE - 1,)),
@@ -300,37 +318,57 @@
         compiler_params=pltpu.CompilerParams(
             collective_id=0, has_side_effects=True, vmem_limit_bytes=48 << 20
         ),
-    )(voltages, taps, table)
-
-
-def correlate_kernel(scale, r_ref, o_ref):
-    m = pl.program_id(0)
-    size = o_ref.shape[2]
-    times = r_ref.shape[0]
-    half = r_ref.shape[2] // 2
-    real = jnp.zeros(o_ref.shape[2:], jnp.float32)
-    imag = jnp.zeros(o_ref.shape[2:], jnp.float32)
-    contract = (((1,), (1,)), ((), ()))
-    at = pl.ds(pl.multiple_of(m * size, size), size)
-    for t in range(times):
-        mine = r_ref[t, at, :]
-        turned = jnp.concatenate([mine[:, half:], -mine[:, :half]], axis=1)
-        every = r_ref[t]
-        real += lax.dot_general(mine, every, contract, preferred_element_type=jnp.float32)
-        imag += lax.dot_general(turned, every, contract, preferred_element_type=jnp.float32)
-    o_ref[0, 0] = real * scale
-    o_ref[0, 1] = imag * scale
-
-
-def correlate(spectra, scale, size=128):
+    )(*operands)
+
+
+def correlate_kernel(scale, r_ref, o_hbm, o, sem):
+    times, inputs, lanes = r_ref.shape
+    half, cut = lanes // 2, inputs // 2
+
+    def product(left, right):
+        return scale * lax.dot_general(
+            left, right, (((1,), (1,)), ((), ())), preferred_element_type=jnp.float32
+        )
+
+    def put(plane, part):
+        at = pl.ds(part * cut, cut)
+        copy = pltpu.make_async_copy(
+            o.at[plane, at], o_hbm.at[0, plane, at], sem.at[2 * plane + part]
+        )
+        copy.start()
+        return copy
+
+    every = jnp.concatenate([r_ref[t] for t in range(times)], axis=1)
+    top = product(every[:cut], every)
+    o[0, :cut, :] = top
+    copies = [put(0, 0)]
+    o[0, cut:, cut:] = product(every[cut:], every[cut:])
+    o[0, cut:, :cut] = top[:, cut:].T
+    copies.append(put(0, 1))
+    real = jnp.concatenate([r_ref[t, :, :half] for t in range(times)], axis=1)
+    imag = jnp.concatenate([r_ref[t, :, half:] for t in range(times)], axis=1)
+    mixed = product(imag, real)
+    turned = mixed.T
+    o[1, :cut] = mixed[:cut] - turned[:cut]
+    copies.append(put(1, 0))
+    o[1, cut:] = mixed[cut:] - turned[cut:]
+    copies.append(put(1, 1))
+    for copy in copies:
+        copy.wait()
+
+
+def correlate(spectra, scale):
     inputs = spectra.shape[1]
     return pl.pallas_call(
         functools.partial(correlate_kernel, scale),
         name="correlate",
-        grid=(inputs // size,),
         out_shape=jax.ShapeDtypeStruct((1, 2, inputs, inputs), jnp.float32),
         in_specs=[pl.BlockSpec(memory_space=pltpu.VMEM)],
-        out_specs=pl.BlockSpec((1, 2, size, inputs), lambda m: (0, 0, m, 0)),
+        out_specs=pl.BlockSpec(memory_space=pltpu.HBM),
+        scratch_shapes=[
+            pltpu.VMEM((2, inputs, inputs), jnp.float32),
+            pltpu.SemaphoreType.DMA((4,)),
+        ],
         compiler_params=pltpu.CompilerParams(vmem_limit_bytes=32 << 20),
     )(spectra)
 

time: 77.2 us -> 66.9 us (0.87)
  Pallas kernels: 73.7 us -> 66.9 us
  local copies, waits for them, and re-layouts: 3.33 us -> 0 us
    pallas_call x1, Pallas kernels: 6.73 us -> 2.52 us  [correlate(): pl.pallas_call(functools.partial(correlate_kernel, scale), name='correlat...]
    unnamed x6 -> x0, local copies, waits for them, and re-layouts: 3.33 us -> none
    pallas_call x1, Pallas kernels: 67 us -> 64.3 us  [exchange(): pl.pallas_call(exchange_kernel, name='exchange', out_shape=jax.ShapeDtype...]
where the time goes in v2:
time: 66.9 us
  Pallas kernels  66.9 us (100%)
    pallas_call x1, Pallas kernels, exchange(): pl.pallas_call(exchange_kernel, name='exchange', out_shape=jax.ShapeDtype...  64.3 us
    pallas_call x1, Pallas kernels, correlate(): pl.pallas_call(functools.partial(correlate_kernel, scale), name='correlat...  2.52 us

profile of v2, /device:TPU:1, one launch (start us, length us, event | category | flops | bytes accessed | tf_op | source)
XLA Modules:
  0.0 66.9 jit_solution(2481965637815408194)
XLA Ops:
  0.0 64.3 %exchange.1 = bf16[2,4,4,4,2,2,8,256]{7,6,5,4,3,2,1,0:T(8,128)(2,1)S(1)} custom-call(bf16[16,65536]{1,0:T(8,128)(2,1)} %v_hbm.1, f32[4,512]{1,0:T(4,128)} %taps_hbm.1, bf16[512,512]{1,0:T(8,128)(2,1)} %constant.2.clone.table_hbm), custom_call_target="tpu_custom_call" | custom-call | tf_op jit(solution)/shard_map/exchange/pallas_call | solution.py:295
  64.4 2.5 %correlate.1 = f32[1,2,512,512]{3,2,1,0:T(8,128)} custom-call(bf16[8,512,256]{2,1,0:T(8,128)(2,1)S(1)} %bitcast.1), custom_call_target="tpu_custom_call" | custom-call | tf_op jit(solution)/shard_map/correlate/pallas_call | solution.py:362

commit v3 on v2

--- a/solution.py
+++ b/solution.py
@@ -14,6 +14,7 @@
 NX, NY, NZ, NC, ZL = 4, 4, 8, 2, 2
 ZH = NZ // ZL
 PLANE = NY * NX * NC
+FAR = NZ // 2
 HALF = 8
 LANES = 128
 PIECES = 4
@@ -42,16 +43,17 @@
 
 
 def dft_rows(width):
-    channel = channel_of_row()
-    phase = (channel[:, None] * np.arange(width)[None, :]) % width
-    angle = phase.astype(np.float32) * np.float32(2.0 * math.pi / width)
-    rows = np.concatenate([np.cos(angle), -np.sin(angle)], axis=0)
-    return rows.astype(ml_dtypes.bfloat16)
+    parts = []
+    for channel in np.split(channel_of_row(), 2):
+        phase = (channel[:, None] * np.arange(width)[None, :]) % width
+        angle = phase.astype(np.float32) * np.float32(2.0 * math.pi / width)
+        parts += [np.cos(angle), -np.sin(angle)]
+    return np.concatenate(parts, axis=0).astype(ml_dtypes.bfloat16)
 
 
 def exchange_kernel(
     v_hbm, taps_hbm, table_hbm, r_ref,
-    v, taps_ref, table_ref, hist, f32s, s32, sa, sb, za, yb,
+    v, taps_ref, table_ref, hist, f32s, s32, sa, sb, za, yb, ta, tb,
     load_sem, hist_send, hist_recv, local_sem,
     za_send, za_recv, xa_send, xa_recv, xb_send, xb_recv, zb_send, zb_recv,
 ):
@@ -61,24 +63,25 @@
     inp = lax.axis_index("inp")
     tms = ZL * NX
     taps_n, width = taps_ref.shape
-    spectra = v.shape[1] // width
-    rows = v.shape[0]
+    spectra = v.shape[2] // width
     piece = spectra // PIECES
-
-    def load(g):
+    tail = (taps_n - 1) * width
+    group = PLANE // 2
+
+    def load(half, g):
         at = pl.ds(pl.multiple_of(g * piece * width, width), piece * width)
-        return pltpu.make_async_copy(v_hbm.at[:, at], v.at[:, at], load_sem.at[g])
-
-    load_taps = pltpu.make_async_copy(taps_hbm, taps_ref, load_sem.at[PIECES])
-    load_table = pltpu.make_async_copy(table_hbm, table_ref, load_sem.at[PIECES + 1])
+        return pltpu.make_async_copy(
+            v_hbm.at[pl.ds(half * HALF, HALF), at], v.at[half, :, at], load_sem.at[half, g]
+        )
+
+    load_taps = pltpu.make_async_copy(taps_hbm, taps_ref, load_sem.at[0, PIECES])
+    load_table = pltpu.make_async_copy(table_hbm, table_ref, load_sem.at[1, PIECES])
     load_taps.start()
-    for g in range(PIECES):
-        load(g).start()
-    load_table.start()
-
-    def z_peer(dz):
-        zz = (z + dz) % NZ
-        return zz, device(x, y, zz, c)
+    for half in range(2):
+        for g in range(PIECES):
+            load(half, g).start()
+        if half == 0:
+            load_table.start()
 
     def plane_peer(i):
         xx = (x + i // (NY * NC)) % NX
@@ -88,87 +91,96 @@
 
     later = (inp, (tm + 1) % tms)
     earlier = (inp, (tm + tms - 1) % tms)
+    beside = (device(x, y, (z + 1) % NZ, c), device(x, y, (z + NZ - 1) % NZ, c))
     barrier = pltpu.get_barrier_semaphore()
-    pl.semaphore_signal(barrier, inc=1, device_id=later, device_id_type=MESH)
-    pl.semaphore_signal(barrier, inc=1, device_id=earlier, device_id_type=MESH)
-    for dz in range(1, NZ):
-        pl.semaphore_signal(barrier, inc=1, device_id=z_peer(dz)[1], device_id_type=MESH)
+    for peer in (earlier, later) + beside:
+        pl.semaphore_signal(barrier, inc=1, device_id=peer, device_id_type=MESH)
 
     def greet(i, _):
         pl.semaphore_signal(barrier, inc=1, device_id=plane_peer(i)[3], device_id_type=MESH)
         return 0
 
     lax.fori_loop(1, PLANE, greet, 0)
-    pl.semaphore_wait(barrier, 2 + NZ - 1 + PLANE - 1)
-
-    history = pltpu.make_async_remote_copy(
-        src_ref=v_hbm.at[:, pl.ds((spectra - (taps_n - 1)) * width, (taps_n - 1) * width)],
-        dst_ref=hist,
-        send_sem=hist_send,
-        recv_sem=hist_recv,
-        device_id=later,
-        device_id_type=MESH,
-    )
-    history.start()
+    pl.semaphore_wait(barrier, 4 + PLANE - 1)
+
+    def history(half):
+        return pltpu.make_async_remote_copy(
+            src_ref=v_hbm.at[pl.ds(half * HALF, HALF), pl.ds(spectra * width - tail, tail)],
+            dst_ref=hist.at[half],
+            send_sem=hist_send.at[half],
+            recv_sem=hist_recv.at[half],
+            device_id=later,
+            device_id_type=MESH,
+        )
+
+    history(0).start()
+    history(1).start()
     load_taps.wait()
 
-    def block(ref, s, q):
+    def block(ref, half, s, q):
         at = pl.multiple_of(s * width + q * LANES, LANES)
-        return ref[:, pl.ds(at, LANES)].astype(jnp.float32)
+        return ref[half, :, pl.ds(at, LANES)].astype(jnp.float32)
 
     def gain(q):
         return [
-            jnp.broadcast_to(taps_ref[t : t + 1, q * LANES : (q + 1) * LANES], (rows, LANES))
+            jnp.broadcast_to(taps_ref[t : t + 1, q * LANES : (q + 1) * LANES], (HALF, LANES))
             for t in range(taps_n)
         ]
 
-    def step(gains, s, q, past):
-        past = past + (block(v, s, q),)
+    def step(gains, half, s, q, past):
+        past = past + (block(v, half, s, q),)
         total = gains[0] * past[0]
         for t in range(1, taps_n):
             total = total + gains[t] * past[t]
-        f32s.at[q][pl.ds(s, rows, stride=PITCH), :] = total
+        f32s.at[q][pl.ds(half * HALF * PITCH + s, HALF, stride=PITCH), :] = total
         return past[1:]
 
-    def filter_piece(g, _):
-        load(g).wait()
+    def filter_half(half):
+        def filter_piece(g, _):
+            load(half, g).wait()
+            for q in range(width // LANES):
+                gains = gain(q)
+                past = tuple(
+                    block(v, half, jnp.maximum(g * piece - k, 0), q)
+                    for k in range(taps_n - 1, 0, -1)
+                )
+                for j in range(piece):
+                    past = step(gains, half, g * piece + j, q, past)
+            return 0
+
+        lax.fori_loop(0, PIECES, filter_piece, 0)
+
+    def first_spectra(half):
+        history(half).wait()
         for q in range(width // LANES):
             gains = gain(q)
             past = tuple(
-                block(v, jnp.maximum(g * piece - k, 0), q) for k in range(taps_n - 1, 0, -1)
+                jnp.where(tm > 0, block(hist, half, s, q), 0.0) for s in range(taps_n - 1)
             )
-            for j in range(piece):
-                past = step(gains, g * piece + j, q, past)
-        return 0
-
-    lax.fori_loop(0, PIECES, filter_piece, 0)
-
-    history.wait()
-    seen = tm > 0
-    for q in range(width // LANES):
-        gains = gain(q)
-        past = tuple(jnp.where(seen, block(hist, s, q), 0.0) for s in range(taps_n - 1))
-        for s in range(taps_n - 1):
-            past = step(gains, s, q, past)
-    load_table.wait()
-
-    def transform(half, out):
+            for s in range(taps_n - 1):
+                past = step(gains, half, s, q, past)
+
+    def transform(half, part, out):
         def filtered(i):
+            at = (half * HALF + i) * PITCH
             return jnp.concatenate(
-                [f32s[q, i * PITCH : i * PITCH + spectra, :] for q in range(width // LANES)],
-                axis=1,
+                [f32s[q, at : at + spectra, :] for q in range(width // LANES)], axis=1
             ).astype(jnp.bfloat16)
 
-        for p in range(HALF // 2):
-            i = half * HALF + 2 * p
+        count = group * NZ
+        for i in range(0, HALF, 2):
             f = jnp.concatenate([filtered(i), filtered(i + 1)], axis=0)
             spec = lax.dot_general(
-                table_ref[...], f, (((1,), (1,)), ((), ())), preferred_element_type=jnp.float32
+                table_ref[part * 2 * count : (part + 1) * 2 * count, :],
+                f,
+                (((1,), (1,)), ((), ())),
+                preferred_element_type=jnp.float32,
             )
             for two in range(2):
                 for plane in range(2):
-                    s32.at[plane][pl.ds(2 * p + two, width // 2, stride=HALF), :] = spec[
-                        plane * (width // 2) : (plane + 1) * (width // 2),
+                    at = pl.ds(part * count * HALF + i + two, count, stride=HALF)
+                    s32.at[plane][at, :] = spec[
+                        plane * count : (plane + 1) * count,
                         two * spectra : (two + 1) * spectra,
                     ]
 
@@ -178,29 +190,67 @@
             out[m] = both.reshape(NZ, HALF, 2 * spectra).astype(jnp.bfloat16)
             return 0
 
-        lax.fori_loop(0, PLANE, pack, 0)
+        lax.fori_loop(part * group, (part + 1) * group, pack, 0)
 
     here = (y * NX + x) * NC + c
 
-    transform(0, sa)
-
-    def za_copy(dz):
-        zz, peer = z_peer(dz)
+    def route(s, d, hop):
+        sign = 1 - 2 * s
+        source = (z + NZ - (hop - 1) * sign) % NZ
+        return source, (source + NZ + d * sign) % NZ
+
+    def za_copy(s, d, hop, part):
+        source, target = route(s, d, hop)
+        at = pl.ds(part * group, group)
+        src = sa.at[at, target] if hop == 1 else ta.at[s, hop - 2, d - 2, at]
+        dst = za.at[source % ZL, source // ZL, at] if hop == d else ta.at[s, hop - 1, d - 2, at]
         return pltpu.make_async_remote_copy(
-            src_ref=sa.at[:, zz],
-            dst_ref=za.at[zl, zh],
-            send_sem=za_send.at[dz - 1],
-            recv_sem=za_recv.at[dz - 1],
-            device_id=peer,
+            src_ref=src,
+            dst_ref=dst,
+            send_sem=za_send.at[s, hop - 1, d - 1, part],
+            recv_sem=za_recv.at[s, hop - 1, d - 1, part],
+            device_id=beside[s],
             device_id_type=MESH,
         )
 
-    for dz in (4, 3, 5, 2, 6, 1, 7):
-        za_copy(dz).start()
+    def zb_copy(s, d, hop):
+        source, target = route(s, d, hop)
+        at = pl.ds(s * (NX // 2), NX // 2) if d == FAR else pl.ds(0, NX)
+        src = yb.at[at, :, :, target] if hop == 1 else tb.at[s, hop - 2, d - 2, at]
+        dst = (
+            r_ref.at[source % ZL, at, :, source // ZL, :, 1]
+            if hop == d
+            else tb.at[s, hop - 1, d - 2, at]
+        )
+        return pltpu.make_async_remote_copy(
+            src_ref=src,
+            dst_ref=dst,
+            send_sem=zb_send.at[s, hop - 1, d - 1],
+            recv_sem=zb_recv.at[s, hop - 1, d - 1],
+            device_id=beside[s],
+            device_id_type=MESH,
+        )
+
+    def legs_a(d):
+        return [(s, part) for part in range(2) for s in range(2) if d < FAR or s == part]
+
+    filter_half(0)
+    filter_half(1)
+    first_spectra(0)
+    load_table.wait()
+
+    for part in range(2):
+        transform(0, part, sa)
+        for d in range(FAR, 0, -1):
+            for s, p in legs_a(d):
+                if p == part:
+                    za_copy(s, d, 1, p).start()
     keep_a = pltpu.make_async_copy(sa.at[:, z], za.at[zl, zh], local_sem.at[0])
     keep_a.start()
 
-    transform(1, sb)
+    first_spectra(1)
+    for part in range(2):
+        transform(1, part, sb)
 
     def xb_copy(i):
         xx, yy, cc, peer = plane_peer(i)
@@ -221,6 +271,12 @@
     keep_b = pltpu.make_async_copy(sb.at[here], yb.at[x, y, c], local_sem.at[1])
     keep_b.start()
 
+    for hop in range(2, FAR + 1):
+        for d in range(FAR, hop - 1, -1):
+            for s, p in legs_a(d):
+                za_copy(s, d, hop - 1, p).wait_recv()
+                za_copy(s, d, hop, p).start()
+
     def xb_wait(i, _):
         xb_copy(i).wait()
         return 0
@@ -228,26 +284,17 @@
     lax.fori_loop(1, PLANE, xb_wait, 0)
     keep_b.wait()
 
-    def zb_copy(dz):
-        zz, peer = z_peer(dz)
-        return pltpu.make_async_remote_copy(
-            src_ref=yb.at[:, :, :, zz],
-            dst_ref=r_ref.at[zl, :, :, zh, :, 1],
-            send_sem=zb_send.at[dz - 1],
-            recv_sem=zb_recv.at[dz - 1],
-            device_id=peer,
-            device_id_type=MESH,
-        )
-
-    for dz in (4, 3, 5, 2, 6, 1, 7):
-        zb_copy(dz).start()
+    for d in range(FAR, 0, -1):
+        for s in range(2):
+            zb_copy(s, d, 1).start()
     last_b = pltpu.make_async_copy(
         yb.at[:, :, :, z], r_ref.at[zl, :, :, zh, :, 1], local_sem.at[2]
     )
     last_b.start()
 
-    for dz in range(1, NZ):
-        za_copy(dz).wait()
+    for d in range(1, FAR + 1):
+        for s, p in legs_a(d):
+            za_copy(s, d, d, p).wait_recv()
     keep_a.wait()
 
     def xa_copy(i):
@@ -271,15 +318,31 @@
     )
     last_a.start()
 
+    for hop in range(2, FAR + 1):
+        for d in range(FAR, hop - 1, -1):
+            for s in range(2):
+                zb_copy(s, d, hop - 1).wait_recv()
+                zb_copy(s, d, hop).start()
+
+    for d in range(1, FAR + 1):
+        for hop in range(1, d + 1):
+            for s, p in legs_a(d):
+                za_copy(s, d, hop, p).wait_send()
+
     def xa_wait(i, _):
         xa_copy(i).wait()
         return 0
 
     lax.fori_loop(1, PLANE, xa_wait, 0)
     last_a.wait()
-    for dz in range(1, NZ):
-        zb_copy(dz).wait()
     last_b.wait()
+    for d in range(1, FAR + 1):
+        for s in range(2):
+            zb_copy(s, d, d).wait_recv()
+    for d in range(1, FAR + 1):
+        for hop in range(1, d + 1):
+            for s in range(2):
+                zb_copy(s, d, hop).wait_send()
 
 
 def exchange(voltages, taps, table):
@@ -299,21 +362,23 @@
         in_specs=[pl.BlockSpec(memory_space=pltpu.HBM)] * 3,
         out_specs=pl.BlockSpec(memory_space=pltpu.VMEM),
         scratch_shapes=[
-            pltpu.VMEM((inp_dev, samples), bf16),
+            pltpu.VMEM((2, HALF, samples), bf16),
             pltpu.VMEM(taps.shape, taps.dtype),
             pltpu.VMEM(table.shape, table.dtype),
-            pltpu.VMEM((inp_dev, (taps.shape[0] - 1) * width), bf16),
+            pltpu.VMEM((2, HALF, (taps.shape[0] - 1) * width), bf16),
             pltpu.VMEM((width // LANES, inp_dev * PITCH, LANES), jnp.float32),
             pltpu.VMEM((2, width // 2 * HALF, spectra), jnp.float32),
             pltpu.VMEM((PLANE, NZ) + block, bf16),
             pltpu.VMEM((PLANE, NZ) + block, bf16),
             pltpu.VMEM((ZL, ZH, PLANE) + block, bf16),
             pltpu.VMEM((NX, NY, NC, NZ) + block, bf16),
-            dma((PIECES + 2,)), dma(()), dma(()), dma((4,)),
-            dma((NZ - 1,)), dma((NZ - 1,)),
+            pltpu.VMEM((2, FAR - 1, FAR - 1, PLANE) + block, bf16),
+            pltpu.VMEM((2, FAR - 1, FAR - 1, NX, NY, NC) + block, bf16),
+            dma((2, PIECES + 1)), dma((2,)), dma((2,)), dma((4,)),
+            dma((2, FAR, FAR, 2)), dma((2, FAR, FAR, 2)),
             dma((PLANE - 1,)), dma((PLANE - 1,)),
             dma((PLANE - 1,)), dma((PLANE - 1,)),
-            dma((NZ - 1,)), dma((NZ - 1,)),
+            dma((2, FAR, FAR)), dma((2, FAR, FAR)),
         ],
         compiler_params=pltpu.CompilerParams(
             collective_id=0, has_side_effects=True, vmem_limit_bytes=48 << 20

time: 66.9 us -> 66.8 us (level)
  no operation moved by 1% of the time
where the time goes in v3:
time: 66.8 us
  Pallas kernels  66.8 us (100%)
    pallas_call x1, Pallas kernels, exchange(): pl.pallas_call(exchange_kernel, name='exchange', out_shape=jax.ShapeDtype...  64.2 us
    pallas_call x1, Pallas kernels, correlate(): pl.pallas_call(functools.partial(correlate_kernel, scale), name='correlat...  2.52 us

profile of v3, /device:TPU:1, one launch (start us, length us, event | category | flops | bytes accessed | tf_op | source)
XLA Modules:
  0.0 66.8 jit_solution(5243056262337198423)
XLA Ops:
  0.0 64.2 %exchange.1 = bf16[2,4,4,4,2,2,8,256]{7,6,5,4,3,2,1,0:T(8,128)(2,1)S(1)} custom-call(bf16[16,65536]{1,0:T(8,128)(2,1)} %v_hbm.1, f32[4,512]{1,0:T(4,128)} %taps_hbm.1, bf16[512,512]{1,0:T(8,128)(2,1)} %constant.2.clone.table_hbm), custom_call_target="tpu_custom_call" | custom-call | tf_op jit(solution)/shard_map/exchange/pallas_call | solution.py:358
  64.2 2.5 %correlate.1 = f32[1,2,512,512]{3,2,1,0:T(8,128)} custom-call(bf16[8,512,256]{2,1,0:T(8,128)(2,1)S(1)} %bitcast.1), custom_call_target="tpu_custom_call" | custom-call | tf_op jit(solution)/shard_map/correlate/pallas_call | solution.py:427

commit v4 on v3

--- a/solution.py
+++ b/solution.py
@@ -32,19 +32,19 @@
 
 
 def channel_of_row():
-    order = np.empty((NY, NX, NC, NZ), np.int64)
-    for y in range(NY):
-        for x in range(NX):
-            for c in range(NC):
-                for z in range(NZ):
+    order = np.empty((NC, NZ, NY, NX), np.int64)
+    for c in range(NC):
+        for z in range(NZ):
+            for y in range(NY):
+                for x in range(NX):
                     inp, tm = device(x, y, z, c)
-                    order[y, x, c, z] = inp * (ZL * NX) + tm
+                    order[c, z, y, x] = inp * (ZL * NX) + tm
     return order.reshape(-1)
 
 
 def dft_rows(width):
     parts = []
-    for channel in np.split(channel_of_row(), 2):
+    for channel in np.split(channel_of_row(), NC):
         phase = (channel[:, None] * np.arange(width)[None, :]) % width
         angle = phase.astype(np.float32) * np.float32(2.0 * math.pi / width)
         parts += [np.cos(angle), -np.sin(angle)]
@@ -53,9 +53,9 @@
 
 def exchange_kernel(
     v_hbm, taps_hbm, table_hbm, r_ref,
-    v, taps_ref, table_ref, hist, f32s, s32, sa, sb, za, yb, ta, tb,
+    v, taps_ref, table_ref, hist, f32s, s32, sa, sb, za, yb, ta, tb, ca, cb, xa, xb, via0, via1,
     load_sem, hist_send, hist_recv, local_sem,
-    za_send, za_recv, xa_send, xa_recv, xb_send, xb_recv, zb_send, zb_recv,
+    ready, core_send, core_recv, za_send, za_recv, zb_send, zb_recv, plane_send, plane_recv,
 ):
     x, y, z, c = position()
     zh, zl = z // ZL, z % ZL
@@ -66,7 +66,7 @@
     spectra = v.shape[2] // width
     piece = spectra // PIECES
     tail = (taps_n - 1) * width
-    group = PLANE // 2
+    count = NZ * NY * NX
 
     def load(half, g):
         at = pl.ds(pl.multiple_of(g * piece * width, width), piece * width)
@@ -83,25 +83,24 @@
         if half == 0:
             load_table.start()
 
-    def plane_peer(i):
-        xx = (x + i // (NY * NC)) % NX
-        yy = (y + (i // NC) % NY) % NY
-        cc = (c + i % NC) % NC
-        return xx, yy, cc, device(xx, yy, z, cc)
-
+    beside = (
+        (device(x, y, (z + 1) % NZ, c), device(x, y, (z + NZ - 1) % NZ, c)),
+        (device((x + 1) % NX, y, z, c), device((x + NX - 1) % NX, y, z, c)),
+        (device(x, (y + 1) % NY, z, c), device(x, (y + NY - 1) % NY, z, c)),
+    )
+    twin = device(x, y, z, 1 - c)
     later = (inp, (tm + 1) % tms)
     earlier = (inp, (tm + tms - 1) % tms)
-    beside = (device(x, y, (z + 1) % NZ, c), device(x, y, (z + NZ - 1) % NZ, c))
+
     barrier = pltpu.get_barrier_semaphore()
-    for peer in (earlier, later) + beside:
+    callers = (beside[0][1], beside[1][1], beside[2][1], twin, earlier)
+    for peer in callers:
         pl.semaphore_signal(barrier, inc=1, device_id=peer, device_id_type=MESH)
-
-    def greet(i, _):
-        pl.semaphore_signal(barrier, inc=1, device_id=plane_peer(i)[3], device_id_type=MESH)
-        return 0
-
-    lax.fori_loop(1, PLANE, greet, 0)
-    pl.semaphore_wait(barrier, 4 + PLANE - 1)
+    pl.semaphore_wait(barrier, len(callers))
+    for axis in range(3):
+        pl.semaphore_signal(
+            ready.at[axis], inc=1, device_id=beside[axis][0], device_id_type=MESH
+        )
 
     def history(half):
         return pltpu.make_async_remote_copy(
@@ -167,7 +166,6 @@
                 [f32s[q, at : at + spectra, :] for q in range(width // LANES)], axis=1
             ).astype(jnp.bfloat16)
 
-        count = group * NZ
         for i in range(0, HALF, 2):
             f = jnp.concatenate([filtered(i), filtered(i + 1)], axis=0)
             spec = lax.dot_general(
@@ -185,51 +183,147 @@
                     ]
 
         def pack(m, _):
-            at = pl.ds(pl.multiple_of(m * NZ * HALF, NZ * HALF), NZ * HALF)
+            size = NY * NX * HALF
+            at = pl.ds(pl.multiple_of((part * NZ + m) * size, size), size)
             both = jnp.concatenate([s32[0, at, :], s32[1, at, :]], axis=1)
-            out[m] = both.reshape(NZ, HALF, 2 * spectra).astype(jnp.bfloat16)
+            out[part, m] = both.reshape(NY, NX, HALF, 2 * spectra).astype(jnp.bfloat16)
             return 0
 
-        lax.fori_loop(part * group, (part + 1) * group, pack, 0)
-
-    here = (y * NX + x) * NC + c
+        lax.fori_loop(0, NZ, pack, 0)
 
     def route(s, d, hop):
         sign = 1 - 2 * s
         source = (z + NZ - (hop - 1) * sign) % NZ
         return source, (source + NZ + d * sign) % NZ
 
-    def za_copy(s, d, hop, part):
-        source, target = route(s, d, hop)
-        at = pl.ds(part * group, group)
-        src = sa.at[at, target] if hop == 1 else ta.at[s, hop - 2, d - 2, at]
-        dst = za.at[source % ZL, source // ZL, at] if hop == d else ta.at[s, hop - 1, d - 2, at]
+    def remote(src, dst, send, recv, peer):
         return pltpu.make_async_remote_copy(
             src_ref=src,
             dst_ref=dst,
-            send_sem=za_send.at[s, hop - 1, d - 1, part],
-            recv_sem=za_recv.at[s, hop - 1, d - 1, part],
-            device_id=beside[s],
+            send_sem=send,
+            recv_sem=recv,
+            device_id=peer,
             device_id_type=MESH,
         )
+
+    def za_copy(s, d, hop, part):
+        source, target = route(s, d, hop)
+        src = sa.at[part, target] if hop == 1 else ta.at[s, hop - 2, d - 2, part]
+        dst = (
+            za.at[part, source % ZL * ZH + source // ZL]
+            if hop == d
+            else ta.at[s, hop - 1, d - 2, part]
+        )
+        at = (s, hop - 1, d - 1, part)
+        return remote(src, dst, za_send.at[at], za_recv.at[at], beside[0][s])
 
     def zb_copy(s, d, hop):
         source, target = route(s, d, hop)
         at = pl.ds(s * (NX // 2), NX // 2) if d == FAR else pl.ds(0, NX)
-        src = yb.at[at, :, :, target] if hop == 1 else tb.at[s, hop - 2, d - 2, at]
+        src = yb.at[at, :, target] if hop == 1 else tb.at[s, hop - 2, d - 2, at]
         dst = (
             r_ref.at[source % ZL, at, :, source // ZL, :, 1]
             if hop == d
             else tb.at[s, hop - 1, d - 2, at]
         )
-        return pltpu.make_async_remote_copy(
-            src_ref=src,
-            dst_ref=dst,
-            send_sem=zb_send.at[s, hop - 1, d - 1],
-            recv_sem=zb_recv.at[s, hop - 1, d - 1],
-            device_id=beside[s],
-            device_id_type=MESH,
-        )
+        at = (s, hop - 1, d - 1)
+        return remote(src, dst, zb_send.at[at], zb_recv.at[at], beside[0][s])
+
+    stage, rings, passing = (ca, cb), (xa, xb), (via0, via1)
+    per = NZ // 2
+
+    def core_copy(half, src):
+        return remote(
+            src.at[1 - c], stage[half].at[:, c], core_send.at[half], core_recv.at[half], twin
+        )
+
+    def own_core(half, src):
+        return pltpu.make_async_copy(
+            src.at[c], stage[half].at[:, c], local_sem.at[half, 0]
+        )
+
+    def leg_src(half, unit, leg, to, lo, n):
+        along_x = unit == leg
+        if leg == 1:
+            return rings[half].at[unit, :, pl.ds(lo, n), :, to]
+        at = pl.ds(unit * per + lo, n)
+        return stage[half].at[at, :, :, to] if along_x else stage[half].at[at, :, to]
+
+    def leg_dst(half, unit, leg, frm, lo, n):
+        along_x = unit == leg
+        if leg == 0:
+            return rings[half].at[unit, frm, pl.ds(lo, n)]
+        if half == 0:
+            at = pl.ds(lo, n)
+            if along_x:
+                return r_ref.at[unit, frm, :, at, :, 0]
+            return r_ref.at[unit, :, frm, at, :, 0]
+        at = pl.ds(unit * per + lo, n)
+        return yb.at[frm, :, at] if along_x else yb.at[:, frm, at]
+
+    def plane_copy(half, unit, leg, s, kind):
+        along_x = unit == leg
+        size, mine = (NX, x) if along_x else (NY, y)
+        sign = 1 - 2 * s
+        lo, n = (0, per) if kind == 0 else (s * per // 2, per // 2)
+        peer = beside[1 if along_x else 2][s]
+        via = passing[leg].at[half, unit, s]
+        if kind == 0:
+            src = leg_src(half, unit, leg, (mine + size + sign) % size, lo, n)
+            dst = leg_dst(half, unit, leg, mine, lo, n)
+        elif kind == 1:
+            src = leg_src(half, unit, leg, (mine + 2) % size, lo, n)
+            dst = via
+        else:
+            src = via
+            dst = leg_dst(half, unit, leg, (mine + size - sign) % size, lo, n)
+        at = (half, unit, leg, s, kind)
+        return remote(src, dst, plane_send.at[at], plane_recv.at[at], peer)
+
+    def own_leg(half, unit, leg):
+        mine = x if unit == leg else y
+        return pltpu.make_async_copy(
+            leg_src(half, unit, leg, mine, 0, per),
+            leg_dst(half, unit, leg, mine, 0, per),
+            local_sem.at[half, 1 + 2 * unit + leg],
+        )
+
+    every_leg = [(unit, s) for unit in range(2) for s in range(2)]
+
+    def legs_start(half, leg, first=False):
+        for s in range(2):
+            if first and s == 1:
+                pl.semaphore_wait(ready.at[1], 1)
+                pl.semaphore_wait(ready.at[2], 1)
+            for kind in (1, 0):
+                for unit in range(2):
+                    plane_copy(half, unit, leg, s, kind).start()
+        for unit in range(2):
+            own_leg(half, unit, leg).start()
+
+    def legs_forward(half, leg):
+        for unit, s in every_leg:
+            plane_copy(half, unit, leg, s, 1).wait_recv()
+            plane_copy(half, unit, leg, s, 2).start()
+
+    def legs_wait(half, leg):
+        for unit, s in every_leg:
+            plane_copy(half, unit, leg, s, 0).wait_recv()
+            plane_copy(half, unit, leg, s, 2).wait_recv()
+        for unit in range(2):
+            own_leg(half, unit, leg).wait()
+
+    def za_forward(hop):
+        for d in range(FAR, hop - 1, -1):
+            for s, p in legs_a(d):
+                za_copy(s, d, hop - 1, p).wait_recv()
+                za_copy(s, d, hop, p).start()
+
+    def zb_forward(hop):
+        for d in range(FAR, hop - 1, -1):
+            for s in range(2):
+                zb_copy(s, d, hop - 1).wait_recv()
+                zb_copy(s, d, hop).start()
 
     def legs_a(d):
         return [(s, part) for part in range(2) for s in range(2) if d < FAR or s == part]
@@ -239,56 +333,39 @@
     first_spectra(0)
     load_table.wait()
 
-    for part in range(2):
+    for part in range(NC):
         transform(0, part, sa)
-        for d in range(FAR, 0, -1):
-            for s, p in legs_a(d):
-                if p == part:
-                    za_copy(s, d, 1, p).start()
-    keep_a = pltpu.make_async_copy(sa.at[:, z], za.at[zl, zh], local_sem.at[0])
+        for s in range(2):
+            if part == 0 and s == 1:
+                pl.semaphore_wait(ready.at[0], 1)
+            for d in range(FAR, 0, -1):
+                if (s, part) in legs_a(d):
+                    za_copy(s, d, 1, part).start()
+    keep_a = pltpu.make_async_copy(sa.at[:, z], za.at[:, zl * ZH + zh], local_sem.at[0, 5])
     keep_a.start()
 
     first_spectra(1)
-    for part in range(2):
+    for part in range(NC):
         transform(1, part, sb)
-
-    def xb_copy(i):
-        xx, yy, cc, peer = plane_peer(i)
-        return pltpu.make_async_remote_copy(
-            src_ref=sb.at[(yy * NX + xx) * NC + cc],
-            dst_ref=yb.at[x, y, c],
-            send_sem=xb_send.at[i - 1],
-            recv_sem=xb_recv.at[i - 1],
-            device_id=peer,
-            device_id_type=MESH,
-        )
-
-    def xb_start(i, _):
-        xb_copy(i).start()
-        return 0
-
-    lax.fori_loop(1, PLANE, xb_start, 0)
-    keep_b = pltpu.make_async_copy(sb.at[here], yb.at[x, y, c], local_sem.at[1])
-    keep_b.start()
-
-    for hop in range(2, FAR + 1):
-        for d in range(FAR, hop - 1, -1):
-            for s, p in legs_a(d):
-                za_copy(s, d, hop - 1, p).wait_recv()
-                za_copy(s, d, hop, p).start()
-
-    def xb_wait(i, _):
-        xb_copy(i).wait()
-        return 0
-
-    lax.fori_loop(1, PLANE, xb_wait, 0)
-    keep_b.wait()
+    core_copy(1, sb).start()
+    own_core(1, sb).start()
+    core_copy(1, sb).wait()
+    own_core(1, sb).wait()
+    legs_start(1, 0, first=True)
+    za_forward(2)
+    legs_forward(1, 0)
+    legs_wait(1, 0)
+    legs_start(1, 1)
+    za_forward(3)
+    legs_forward(1, 1)
+    za_forward(4)
+    legs_wait(1, 1)
 
     for d in range(FAR, 0, -1):
         for s in range(2):
             zb_copy(s, d, 1).start()
     last_b = pltpu.make_async_copy(
-        yb.at[:, :, :, z], r_ref.at[zl, :, :, zh, :, 1], local_sem.at[2]
+        yb.at[:, :, z], r_ref.at[zl, :, :, zh, :, 1], local_sem.at[1, 5]
     )
     last_b.start()
 
@@ -296,45 +373,29 @@
         for s, p in legs_a(d):
             za_copy(s, d, d, p).wait_recv()
     keep_a.wait()
-
-    def xa_copy(i):
-        xx, yy, cc, peer = plane_peer(i)
-        return pltpu.make_async_remote_copy(
-            src_ref=za.at[:, :, (yy * NX + xx) * NC + cc],
-            dst_ref=r_ref.at[:, x, y, :, c, 0],
-            send_sem=xa_send.at[i - 1],
-            recv_sem=xa_recv.at[i - 1],
-            device_id=peer,
-            device_id_type=MESH,
-        )
-
-    def xa_start(i, _):
-        xa_copy(i).start()
-        return 0
-
-    lax.fori_loop(1, PLANE, xa_start, 0)
-    last_a = pltpu.make_async_copy(
-        za.at[:, :, here], r_ref.at[:, x, y, :, c, 0], local_sem.at[3]
-    )
-    last_a.start()
-
-    for hop in range(2, FAR + 1):
-        for d in range(FAR, hop - 1, -1):
-            for s in range(2):
-                zb_copy(s, d, hop - 1).wait_recv()
-                zb_copy(s, d, hop).start()
+    core_copy(0, za).start()
+    own_core(0, za).start()
+    core_copy(0, za).wait()
+    own_core(0, za).wait()
+    legs_start(0, 0)
+    zb_forward(2)
+    legs_forward(0, 0)
+    legs_wait(0, 0)
+    legs_start(0, 1)
+    zb_forward(3)
+    legs_forward(0, 1)
+    zb_forward(4)
 
     for d in range(1, FAR + 1):
         for hop in range(1, d + 1):
             for s, p in legs_a(d):
                 za_copy(s, d, hop, p).wait_send()
-
-    def xa_wait(i, _):
-        xa_copy(i).wait()
-        return 0
-
-    lax.fori_loop(1, PLANE, xa_wait, 0)
-    last_a.wait()
+    for half in (1, 0):
+        for leg in range(2):
+            for unit, s in every_leg:
+                for kind in range(3):
+                    plane_copy(half, unit, leg, s, kind).wait_send()
+    legs_wait(0, 1)
     last_b.wait()
     for d in range(1, FAR + 1):
         for s in range(2):
@@ -368,17 +429,23 @@
             pltpu.VMEM((2, HALF, (taps.shape[0] - 1) * width), bf16),
             pltpu.VMEM((width // LANES, inp_dev * PITCH, LANES), jnp.float32),
             pltpu.VMEM((2, width // 2 * HALF, spectra), jnp.float32),
-            pltpu.VMEM((PLANE, NZ) + block, bf16),
-            pltpu.VMEM((PLANE, NZ) + block, bf16),
-            pltpu.VMEM((ZL, ZH, PLANE) + block, bf16),
-            pltpu.VMEM((NX, NY, NC, NZ) + block, bf16),
-            pltpu.VMEM((2, FAR - 1, FAR - 1, PLANE) + block, bf16),
+            pltpu.VMEM((NC, NZ, NY, NX) + block, bf16),
+            pltpu.VMEM((NC, NZ, NY, NX) + block, bf16),
+            pltpu.VMEM((NC, NZ, NY, NX) + block, bf16),
+            pltpu.VMEM((NX, NY, NZ, NC) + block, bf16),
+            pltpu.VMEM((2, FAR - 1, FAR - 1, NC, NY, NX) + block, bf16),
             pltpu.VMEM((2, FAR - 1, FAR - 1, NX, NY, NC) + block, bf16),
-            dma((2, PIECES + 1)), dma((2,)), dma((2,)), dma((4,)),
-            dma((2, FAR, FAR, 2)), dma((2, FAR, FAR, 2)),
-            dma((PLANE - 1,)), dma((PLANE - 1,)),
-            dma((PLANE - 1,)), dma((PLANE - 1,)),
+            pltpu.VMEM((NZ, NC, NY, NX) + block, bf16),
+            pltpu.VMEM((NZ, NC, NY, NX) + block, bf16),
+            pltpu.VMEM((2, NX, NZ // 2, NC, NY) + block, bf16),
+            pltpu.VMEM((2, NX, NZ // 2, NC, NY) + block, bf16),
+            pltpu.VMEM((2, 2, 2, NZ // 4, NC, NY) + block, bf16),
+            pltpu.VMEM((2, 2, 2, NX, NZ // 4, NC) + block, bf16),
+            dma((2, PIECES + 1)), dma((2,)), dma((2,)), dma((2, 6)),
+            pltpu.SemaphoreType.REGULAR((3,)), dma((2,)), dma((2,)),
+            dma((2, FAR, FAR, NC)), dma((2, FAR, FAR, NC)),
             dma((2, FAR, FAR)), dma((2, FAR, FAR)),
+            dma((2, 2, 2, 2, 3)), dma((2, 2, 2, 2, 3)),
         ],
         compiler_params=pltpu.CompilerParams(
             collective_id=0, has_side_effects=True, vmem_limit_bytes=48 << 20

time: 66.8 us -> 64.5 us (0.966)
  the two profiles are of different devices: /device:TPU:1 before, /device:TPU:8 now
where the time goes in v4:
time: 64.5 us; the launch traced here: 64.4 us
  Pallas kernels  64.4 us (100%)
    pallas_call x1, Pallas kernels, exchange(): pl.pallas_call(exchange_kernel, name='exchange', out_shape=jax.ShapeDtype...  61.8 us
    pallas_call x1, Pallas kernels, correlate(): pl.pallas_call(functools.partial(correlate_kernel, scale), name='correlat...  2.52 us

profile of v4, /device:TPU:8, one launch (start us, length us, event | category | flops | bytes accessed | tf_op | source)
XLA Modules:
  0.0 64.4 jit_solution(17058170680417933090)
XLA Ops:
  0.0 61.8 %exchange.1 = bf16[2,4,4,4,2,2,8,256]{7,6,5,4,3,2,1,0:T(8,128)(2,1)S(1)} custom-call(bf16[16,65536]{1,0:T(8,128)(2,1)} %v_hbm.1, f32[4,512]{1,0:T(4,128)} %taps_hbm.1, bf16[512,512]{1,0:T(8,128)(2,1)} %constant.2.clone.table_hbm), custom_call_target="tpu_custom_call" | custom-call | tf_op jit(solution)/shard_map/exchange/pallas_call | solution.py:419
  61.9 2.5 %correlate.1 = f32[1,2,512,512]{3,2,1,0:T(8,128)} custom-call(bf16[8,512,256]{2,1,0:T(8,128)(2,1)S(1)} %bitcast.1), custom_call_target="tpu_custom_call" | custom-call | tf_op jit(solution)/shard_map/correlate/pallas_call | solution.py:494

commit v5 on v4

--- a/solution.py
+++ b/solution.py
@@ -15,9 +15,8 @@
 ZH = NZ // ZL
 PLANE = NY * NX * NC
 FAR = NZ // 2
-HALF = 8
 LANES = 128
-PIECES = 4
+PIECES = 8
 PITCH = 136
 
 
@@ -51,8 +50,28 @@
     return np.concatenate(parts, axis=0).astype(ml_dtypes.bfloat16)
 
 
+def products(ref):
+    inputs = NY * ZH * NC * ref.shape[5]
+    cut = inputs // 2
+    times = [ref[t // NX, t % NX].reshape(inputs, LANES) for t in range(ZL * NX)]
+    every = jnp.concatenate(times, axis=1)
+    half = LANES // 2
+    turned = jnp.concatenate(
+        [part for t in times for part in (t[:, half:], -t[:, :half])], axis=1
+    )
+    for plane, left in ((0, every), (1, turned)):
+        for low in (False, True):
+            at = slice(cut, inputs) if low else slice(0, cut)
+            yield plane, low, lax.dot_general(
+                left[at],
+                every[cut:] if low else every,
+                (((1,), (1,)), ((), ())),
+                preferred_element_type=jnp.float32,
+            )
+
+
 def exchange_kernel(
-    v_hbm, taps_hbm, table_hbm, r_ref,
+    v_hbm, taps_hbm, table_hbm, rb, sums, ra,
     v, taps_ref, table_ref, hist, f32s, s32, sa, sb, za, yb, ta, tb, ca, cb, xa, xb, via0, via1,
     load_sem, hist_send, hist_recv, local_sem,
     ready, core_send, core_recv, za_send, za_recv, zb_send, zb_recv, plane_send, plane_recv,
@@ -63,25 +82,27 @@
     inp = lax.axis_index("inp")
     tms = ZL * NX
     taps_n, width = taps_ref.shape
-    spectra = v.shape[2] // width
+    rows = v.shape[0]
+    spectra = v.shape[1] // width
     piece = spectra // PIECES
+    span = spectra // 2
     tail = (taps_n - 1) * width
     count = NZ * NY * NX
-
-    def load(half, g):
+    cut = sums.shape[1] // 2
+
+    def load(g):
         at = pl.ds(pl.multiple_of(g * piece * width, width), piece * width)
-        return pltpu.make_async_copy(
-            v_hbm.at[pl.ds(half * HALF, HALF), at], v.at[half, :, at], load_sem.at[half, g]
-        )
-
-    load_taps = pltpu.make_async_copy(taps_hbm, taps_ref, load_sem.at[0, PIECES])
-    load_table = pltpu.make_async_copy(table_hbm, table_ref, load_sem.at[1, PIECES])
+        return pltpu.make_async_copy(v_hbm.at[:, at], v.at[:, at], load_sem.at[g])
+
+    load_taps = pltpu.make_async_copy(taps_hbm, taps_ref, load_sem.at[PIECES])
+    load_table = pltpu.make_async_copy(table_hbm, table_ref, load_sem.at[PIECES + 1])
+    middle = PIECES // 2
     load_taps.start()
-    for half in range(2):
-        for g in range(PIECES):
-            load(half, g).start()
-        if half == 0:
-            load_table.start()
+    for g in range(middle - 1, PIECES):
+        load(g).start()
+    load_table.start()
+    for g in range(middle - 1):
+        load(g).start()
 
     beside = (
         (device(x, y, (z + 1) % NZ, c), device(x, y, (z + NZ - 1) % NZ, c)),
@@ -102,91 +123,89 @@
             ready.at[axis], inc=1, device_id=beside[axis][0], device_id_type=MESH
         )
 
-    def history(half):
-        return pltpu.make_async_remote_copy(
-            src_ref=v_hbm.at[pl.ds(half * HALF, HALF), pl.ds(spectra * width - tail, tail)],
-            dst_ref=hist.at[half],
-            send_sem=hist_send.at[half],
-            recv_sem=hist_recv.at[half],
-            device_id=later,
-            device_id_type=MESH,
-        )
-
-    history(0).start()
-    history(1).start()
+    history = pltpu.make_async_remote_copy(
+        src_ref=v_hbm.at[:, pl.ds(spectra * width - tail, tail)],
+        dst_ref=hist,
+        send_sem=hist_send,
+        recv_sem=hist_recv,
+        device_id=later,
+        device_id_type=MESH,
+    )
+    history.start()
     load_taps.wait()
 
-    def block(ref, half, s, q):
+    def block(ref, s, q):
         at = pl.multiple_of(s * width + q * LANES, LANES)
-        return ref[half, :, pl.ds(at, LANES)].astype(jnp.float32)
+        return ref[:, pl.ds(at, LANES)].astype(jnp.float32)
 
     def gain(q):
         return [
-            jnp.broadcast_to(taps_ref[t : t + 1, q * LANES : (q + 1) * LANES], (HALF, LANES))
+            jnp.broadcast_to(taps_ref[t : t + 1, q * LANES : (q + 1) * LANES], (rows, LANES))
             for t in range(taps_n)
         ]
 
-    def step(gains, half, s, q, past):
-        past = past + (block(v, half, s, q),)
+    def step(gains, s, q, past):
+        past = past + (block(v, s, q),)
         total = gains[0] * past[0]
         for t in range(1, taps_n):
             total = total + gains[t] * past[t]
-        f32s.at[q][pl.ds(half * HALF * PITCH + s, HALF, stride=PITCH), :] = total
+        f32s.at[q][pl.ds(s, rows, stride=PITCH), :] = total
         return past[1:]
 
-    def filter_half(half):
+    def filter_pieces(lo, hi, wait):
         def filter_piece(g, _):
-            load(half, g).wait()
+            if wait:
+                load(g).wait()
             for q in range(width // LANES):
                 gains = gain(q)
                 past = tuple(
-                    block(v, half, jnp.maximum(g * piece - k, 0), q)
-                    for k in range(taps_n - 1, 0, -1)
+                    block(v, jnp.maximum(g * piece - k, 0), q) for k in range(taps_n - 1, 0, -1)
                 )
                 for j in range(piece):
-                    past = step(gains, half, g * piece + j, q, past)
+                    past = step(gains, g * piece + j, q, past)
             return 0
 
-        lax.fori_loop(0, PIECES, filter_piece, 0)
-
-    def first_spectra(half):
-        history(half).wait()
+        lax.fori_loop(lo, hi, filter_piece, 0)
+
+    def first_spectra():
+        history.wait()
         for q in range(width // LANES):
             gains = gain(q)
-            past = tuple(
-                jnp.where(tm > 0, block(hist, half, s, q), 0.0) for s in range(taps_n - 1)
-            )
+            past = tuple(jnp.where(tm > 0, block(hist, s, q), 0.0) for s in range(taps_n - 1))
             for s in range(taps_n - 1):
-                past = step(gains, half, s, q, past)
+                past = step(gains, s, q, past)
 
     def transform(half, part, out):
+        first = lax.broadcasted_iota(jnp.int32, (count, LANES), 1) < span
+
         def filtered(i):
-            at = (half * HALF + i) * PITCH
+            at = i * PITCH + (1 - half) * span
             return jnp.concatenate(
-                [f32s[q, at : at + spectra, :] for q in range(width // LANES)], axis=1
+                [f32s[q, at : at + span, :] for q in range(width // LANES)], axis=1
             ).astype(jnp.bfloat16)
 
-        for i in range(0, HALF, 2):
-            f = jnp.concatenate([filtered(i), filtered(i + 1)], axis=0)
+        for i in range(0, rows, 4):
             spec = lax.dot_general(
                 table_ref[part * 2 * count : (part + 1) * 2 * count, :],
-                f,
+                jnp.concatenate([filtered(i + k) for k in range(4)], axis=0),
                 (((1,), (1,)), ((), ())),
                 preferred_element_type=jnp.float32,
             )
             for two in range(2):
-                for plane in range(2):
-                    at = pl.ds(part * count * HALF + i + two, count, stride=HALF)
-                    s32.at[plane][at, :] = spec[
-                        plane * count : (plane + 1) * count,
-                        two * spectra : (two + 1) * spectra,
-                    ]
+                real = spec[:count, two * LANES : (two + 1) * LANES]
+                imag = spec[count:, two * LANES : (two + 1) * LANES]
+                pairs = (
+                    jnp.where(first, real, pltpu.roll(imag, span, 1)),
+                    jnp.where(first, pltpu.roll(real, span, 1), imag),
+                )
+                for k in range(2):
+                    at = pl.ds(part * count * rows + i + 2 * two + k, count, stride=rows)
+                    s32[at, :] = pairs[k]
 
         def pack(m, _):
-            size = NY * NX * HALF
+            size = NY * NX * rows
             at = pl.ds(pl.multiple_of((part * NZ + m) * size, size), size)
-            both = jnp.concatenate([s32[0, at, :], s32[1, at, :]], axis=1)
-            out[part, m] = both.reshape(NY, NX, HALF, 2 * spectra).astype(jnp.bfloat16)
+            out[part, m] = s32[at, :].reshape(NY, NX, rows, LANES).astype(jnp.bfloat16)
             return 0
 
         lax.fori_loop(0, NZ, pack, 0)
@@ -222,7 +241,7 @@
         at = pl.ds(s * (NX // 2), NX // 2) if d == FAR else pl.ds(0, NX)
         src = yb.at[at, :, target] if hop == 1 else tb.at[s, hop - 2, d - 2, at]
         dst = (
-            r_ref.at[source % ZL, at, :, source // ZL, :, 1]
+            rb.at[source % ZL, at, :, source // ZL]
             if hop == d
             else tb.at[s, hop - 1, d - 2, at]
         )
@@ -256,8 +275,8 @@
         if half == 0:
             at = pl.ds(lo, n)
             if along_x:
-                return r_ref.at[unit, frm, :, at, :, 0]
-            return r_ref.at[unit, :, frm, at, :, 0]
+                return ra.at[unit, frm, :, at]
+            return ra.at[unit, :, frm, at]
         at = pl.ds(unit * per + lo, n)
         return yb.at[frm, :, at] if along_x else yb.at[:, frm, at]
 
@@ -328,9 +347,8 @@
     def legs_a(d):
         return [(s, part) for part in range(2) for s in range(2) if d < FAR or s == part]
 
-    filter_half(0)
-    filter_half(1)
-    first_spectra(0)
+    load(middle - 1).wait()
+    filter_pieces(middle, PIECES, True)
     load_table.wait()
 
     for part in range(NC):
@@ -344,7 +362,10 @@
     keep_a = pltpu.make_async_copy(sa.at[:, z], za.at[:, zl * ZH + zh], local_sem.at[0, 5])
     keep_a.start()
 
-    first_spectra(1)
+    for g in range(middle - 1):
+        load(g).wait()
+    filter_pieces(0, middle, False)
+    first_spectra()
     for part in range(NC):
         transform(1, part, sb)
     core_copy(1, sb).start()
@@ -365,7 +386,7 @@
         for s in range(2):
             zb_copy(s, d, 1).start()
     last_b = pltpu.make_async_copy(
-        yb.at[:, :, z], r_ref.at[zl, :, :, zh, :, 1], local_sem.at[1, 5]
+        yb.at[:, :, z], rb.at[zl, :, :, zh], local_sem.at[1, 5]
     )
     last_b.start()
 
@@ -386,6 +407,12 @@
     legs_forward(0, 1)
     zb_forward(4)
 
+    legs_wait(0, 1)
+    for plane, low, value in products(ra):
+        if low:
+            sums[plane, cut:, cut:] = value
+        else:
+            sums[plane, :cut, :] = value
     for d in range(1, FAR + 1):
         for hop in range(1, d + 1):
             for s, p in legs_a(d):
@@ -395,7 +422,6 @@
             for unit, s in every_leg:
                 for kind in range(3):
                     plane_copy(half, unit, leg, s, kind).wait_send()
-    legs_wait(0, 1)
     last_b.wait()
     for d in range(1, FAR + 1):
         for s in range(2):
@@ -407,41 +433,47 @@
 
 
 def exchange(voltages, taps, table):
-    inp_dev, samples = voltages.shape
+    rows, samples = voltages.shape
     width = taps.shape[1]
-    spectra = samples // width
-    block = (HALF, 2 * spectra)
-    bf16 = jnp.bfloat16
+    inputs = rows * lax.axis_size("inp")
+    block = (rows, LANES)
+    bf16, f32 = jnp.bfloat16, jnp.float32
     dma = pltpu.SemaphoreType.DMA
+    vmem = pltpu.VMEM
     operands = [
         pltpu.with_memory_space_constraint(a, pltpu.HBM) for a in (voltages, taps, table)
     ]
+    gathered = (ZL, NX, NY, ZH, NC) + block
     return pl.pallas_call(
         exchange_kernel,
         name="exchange",
-        out_shape=jax.ShapeDtypeStruct((ZL, NX, NY, ZH, NC, inp_dev // HALF) + block, bf16),
+        out_shape=(
+            jax.ShapeDtypeStruct(gathered, bf16),
+            jax.ShapeDtypeStruct((2, inputs, inputs), f32),
+        ),
         in_specs=[pl.BlockSpec(memory_space=pltpu.HBM)] * 3,
-        out_specs=pl.BlockSpec(memory_space=pltpu.VMEM),
+        out_specs=(pl.BlockSpec(memory_space=vmem),) * 2,
         scratch_shapes=[
-            pltpu.VMEM((2, HALF, samples), bf16),
-            pltpu.VMEM(taps.shape, taps.dtype),
-            pltpu.VMEM(table.shape, table.dtype),
-            pltpu.VMEM((2, HALF, (taps.shape[0] - 1) * width), bf16),
-            pltpu.VMEM((width // LANES, inp_dev * PITCH, LANES), jnp.float32),
-            pltpu.VMEM((2, width // 2 * HALF, spectra), jnp.float32),
-            pltpu.VMEM((NC, NZ, NY, NX) + block, bf16),
-            pltpu.VMEM((NC, NZ, NY, NX) + block, bf16),
-            pltpu.VMEM((NC, NZ, NY, NX) + block, bf16),
-            pltpu.VMEM((NX, NY, NZ, NC) + block, bf16),
-            pltpu.VMEM((2, FAR - 1, FAR - 1, NC, NY, NX) + block, bf16),
-            pltpu.VMEM((2, FAR - 1, FAR - 1, NX, NY, NC) + block, bf16),
-            pltpu.VMEM((NZ, NC, NY, NX) + block, bf16),
-            pltpu.VMEM((NZ, NC, NY, NX) + block, bf16),
-            pltpu.VMEM((2, NX, NZ // 2, NC, NY) + block, bf16),
-            pltpu.VMEM((2, NX, NZ // 2, NC, NY) + block, bf16),
-            pltpu.VMEM((2, 2, 2, NZ // 4, NC, NY) + block, bf16),
-            pltpu.VMEM((2, 2, 2, NX, NZ // 4, NC) + block, bf16),
-            dma((2, PIECES + 1)), dma((2,)), dma((2,)), dma((2, 6)),
+            vmem(gathered, bf16),
+            vmem((rows, samples), bf16),
+            vmem(taps.shape, taps.dtype),
+            vmem(table.shape, table.dtype),
+            vmem((rows, (taps.shape[0] - 1) * width), bf16),
+            vmem((width // LANES, rows * PITCH, LANES), f32),
+            vmem((width // 2 * rows, LANES), f32),
+            vmem((NC, NZ, NY, NX) + block, bf16),
+            vmem((NC, NZ, NY, NX) + block, bf16),
+            vmem((NC, NZ, NY, NX) + block, bf16),
+            vmem((NX, NY, NZ, NC) + block, bf16),
+            vmem((2, FAR - 1, FAR - 1, NC, NY, NX) + block, bf16),
+            vmem((2, FAR - 1, FAR - 1, NX, NY, NC) + block, bf16),
+            vmem((NZ, NC, NY, NX) + block, bf16),
+            vmem((NZ, NC, NY, NX) + block, bf16),
+            vmem((2, NX, NZ // 2, NC, NY) + block, bf16),
+            vmem((2, NX, NZ // 2, NC, NY) + block, bf16),
+            vmem((2, 2, 2, NZ // 4, NC, NY) + block, bf16),
+            vmem((2, 2, 2, NX, NZ // 4, NC) + block, bf16),
+            dma((PIECES + 2,)), dma(()), dma(()), dma((2, 6)),
             pltpu.SemaphoreType.REGULAR((3,)), dma((2,)), dma((2,)),
             dma((2, FAR, FAR, NC)), dma((2, FAR, FAR, NC)),
             dma((2, FAR, FAR)), dma((2, FAR, FAR)),
@@ -453,14 +485,9 @@
     )(*operands)
 
 
-def correlate_kernel(scale, r_ref, o_hbm, o, sem):
-    times, inputs, lanes = r_ref.shape
-    half, cut = lanes // 2, inputs // 2
-
-    def product(left, right):
-        return scale * lax.dot_general(
-            left, right, (((1,), (1,)), ((), ())), preferred_element_type=jnp.float32
-        )
+def correlate_kernel(scale, r_ref, sums, o_hbm, o, sem):
+    cut = sums.shape[1] // 2
+    copies = []
 
     def put(plane, part):
         at = pl.ds(part * cut, cut)
@@ -468,51 +495,42 @@
             o.at[plane, at], o_hbm.at[0, plane, at], sem.at[2 * plane + part]
         )
         copy.start()
-        return copy
-
-    every = jnp.concatenate([r_ref[t] for t in range(times)], axis=1)
-    top = product(every[:cut], every)
-    o[0, :cut, :] = top
-    copies = [put(0, 0)]
-    o[0, cut:, cut:] = product(every[cut:], every[cut:])
-    o[0, cut:, :cut] = top[:, cut:].T
-    copies.append(put(0, 1))
-    real = jnp.concatenate([r_ref[t, :, :half] for t in range(times)], axis=1)
-    imag = jnp.concatenate([r_ref[t, :, half:] for t in range(times)], axis=1)
-    mixed = product(imag, real)
-    turned = mixed.T
-    o[1, :cut] = mixed[:cut] - turned[:cut]
-    copies.append(put(1, 0))
-    o[1, cut:] = mixed[cut:] - turned[cut:]
-    copies.append(put(1, 1))
+        copies.append(copy)
+
+    for plane, low, value in products(r_ref):
+        if low:
+            o[plane, cut:, cut:] = (sums[plane, cut:, cut:] + value) * scale
+        else:
+            top = (sums[plane, :cut, :] + value) * scale
+            o[plane, :cut, :] = top
+            corner = top[:, cut:].T
+            o[plane, cut:, :cut] = -corner if plane else corner
+        put(plane, int(low))
     for copy in copies:
         copy.wait()
 
 
-def correlate(spectra, scale):
-    inputs = spectra.shape[1]
+def correlate(spectra, sums, scale):
+    inputs = sums.shape[1]
     return pl.pallas_call(
         functools.partial(correlate_kernel, scale),
         name="correlate",
         out_shape=jax.ShapeDtypeStruct((1, 2, inputs, inputs), jnp.float32),
-        in_specs=[pl.BlockSpec(memory_space=pltpu.VMEM)],
+        in_specs=[pl.BlockSpec(memory_space=pltpu.VMEM)] * 2,
         out_specs=pl.BlockSpec(memory_space=pltpu.HBM),
         scratch_shapes=[
             pltpu.VMEM((2, inputs, inputs), jnp.float32),
             pltpu.SemaphoreType.DMA((4,)),
         ],
         compiler_params=pltpu.CompilerParams(vmem_limit_bytes=32 << 20),
-    )(spectra)
+    )(spectra, sums)
 
 
 def local(voltages, taps):
     width = taps.shape[1]
     table = jnp.asarray(dft_rows(width))
-    times = lax.axis_size("tm")
-    spectra = voltages.shape[1] // width
-    scale = 1.0 / (spectra * times * width)
-    gathered = exchange(voltages, taps, table)
-    return correlate(gathered.reshape(times, -1, 2 * spectra), scale)
+    scale = 1.0 / (voltages.shape[1] * lax.axis_size("tm"))
+    return correlate(*exchange(voltages, taps, table), scale)
 
 
 def solution(mesh):

time: 64.5 us -> 61.3 us (0.950)
  Pallas kernels: 64.4 us -> 61.2 us
    pallas_call x1, Pallas kernels: 61.8 us -> 59.1 us  [exchange(): pl.pallas_call(exchange_kernel, name='exchange', out_shape=(jax.ShapeDtyp...]
where the time goes in v5:
time: 61.3 us; the launch traced here: 61.2 us
  Pallas kernels  61.2 us (100%)
    pallas_call x1, Pallas kernels, exchange(): pl.pallas_call(exchange_kernel, name='exchange', out_shape=(jax.ShapeDtyp...  59.1 us
    pallas_call x1, Pallas kernels, correlate(): pl.pallas_call(functools.partial(correlate_kernel, scale), name='correlat...  2.13 us

profile of v5, /device:TPU:8, one launch (start us, length us, event | category | flops | bytes accessed | tf_op | source)
XLA Modules:
  0.0 61.2 jit_solution(16284408875879876776)
XLA Ops:
  0.0 59.1 %exchange.1 = (bf16[2,4,4,4,2,16,128]{6,5,4,3,2,1,0:T(8,128)(2,1)S(1)}, f32[2,512,512]{2,1,0:T(8,128)S(1)}) custom-call(bf16[16,65536]{1,0:T(8,128)(2,1)} %v_hbm.1, f32[4,512]{1,0:T(4,128)} %taps_hbm.1, bf16[512,512]{1,0:T(8,128)(2,1)} %constant.2.clone.table_hbm), custom_call_target="tpu_custom_call" | custom-call | tf_op jit(solution)/shard_map/exchange/pallas_call | solution.py:447
  59.1 2.1 %correlate.1 = f32[1,2,512,512]{3,2,1,0:T(8,128)} custom-call(bf16[2,4,4,4,2,16,128]{6,5,4,3,2,1,0:T(8,128)(2,1)S(1)} %get-tuple-element.7.r_ref, f32[2,512,512]{2,1,0:T(8,128)S(1)} %get-tuple-element.8.sums), custom_call_target="tpu_custom_call" | custom-call | tf_op jit(solution)/shard_map/correlate/pallas_call | solution.py:515

commit v6 on v5

--- a/solution.py
+++ b/solution.py
@@ -50,10 +50,10 @@
     return np.concatenate(parts, axis=0).astype(ml_dtypes.bfloat16)
 
 
-def products(ref):
-    inputs = NY * ZH * NC * ref.shape[5]
+def products(times):
+    inputs = math.prod(times[0].shape[:-1])
     cut = inputs // 2
-    times = [ref[t // NX, t % NX].reshape(inputs, LANES) for t in range(ZL * NX)]
+    times = [t.reshape(inputs, LANES) for t in times]
     every = jnp.concatenate(times, axis=1)
     half = LANES // 2
     turned = jnp.concatenate(
@@ -71,7 +71,7 @@
 
 
 def exchange_kernel(
-    v_hbm, taps_hbm, table_hbm, rb, sums, ra,
+    v_hbm, taps_hbm, table_hbm, rb, sums, ra, rc,
     v, taps_ref, table_ref, hist, f32s, s32, sa, sb, za, yb, ta, tb, ca, cb, xa, xb, via0, via1,
     load_sem, hist_send, hist_recv, local_sem,
     ready, core_send, core_recv, za_send, za_recv, zb_send, zb_recv, plane_send, plane_recv,
@@ -95,12 +95,19 @@
         return pltpu.make_async_copy(v_hbm.at[:, at], v.at[:, at], load_sem.at[g])
 
     load_taps = pltpu.make_async_copy(taps_hbm, taps_ref, load_sem.at[PIECES])
-    load_table = pltpu.make_async_copy(table_hbm, table_ref, load_sem.at[PIECES + 1])
+
+    def load_table(part):
+        at = pl.ds(part * 2 * count, 2 * count)
+        return pltpu.make_async_copy(
+            table_hbm.at[at], table_ref.at[at], load_sem.at[PIECES + 1 + part]
+        )
+
     middle = PIECES // 2
     load_taps.start()
     for g in range(middle - 1, PIECES):
         load(g).start()
-    load_table.start()
+    for part in range(NC):
+        load_table(part).start()
     for g in range(middle - 1):
         load(g).start()
 
@@ -241,7 +248,7 @@
         at = pl.ds(s * (NX // 2), NX // 2) if d == FAR else pl.ds(0, NX)
         src = yb.at[at, :, target] if hop == 1 else tb.at[s, hop - 2, d - 2, at]
         dst = (
-            rb.at[source % ZL, at, :, source // ZL]
+            (rb if d % ZL else rc).at[at, :, source // ZL]
             if hop == d
             else tb.at[s, hop - 1, d - 2, at]
         )
@@ -349,9 +356,9 @@
 
     load(middle - 1).wait()
     filter_pieces(middle, PIECES, True)
-    load_table.wait()
 
     for part in range(NC):
+        load_table(part).wait()
         transform(0, part, sa)
         for s in range(2):
             if part == 0 and s == 1:
@@ -382,11 +389,11 @@
     za_forward(4)
     legs_wait(1, 1)
 
-    for d in range(FAR, 0, -1):
+    for d in range(FAR, 1, -1):
         for s in range(2):
             zb_copy(s, d, 1).start()
     last_b = pltpu.make_async_copy(
-        yb.at[:, :, z], rb.at[zl, :, :, zh], local_sem.at[1, 5]
+        yb.at[:, :, z], rc.at[:, :, zh], local_sem.at[1, 5]
     )
     last_b.start()
 
@@ -406,13 +413,17 @@
     zb_forward(3)
     legs_forward(0, 1)
     zb_forward(4)
+    for s in range(2):
+        zb_copy(s, 1, 1).start()
 
     legs_wait(0, 1)
-    for plane, low, value in products(ra):
-        if low:
-            sums[plane, cut:, cut:] = value
-        else:
-            sums[plane, :cut, :] = value
+    def gather(ref):
+        return [ref[t] for t in range(NX)]
+
+    for plane, low, value in products(gather(ra.at[0]) + gather(ra.at[1])):
+        at = (plane, slice(cut, None), slice(cut, None)) if low else (plane, slice(0, cut))
+        sums[at] = value
+
     for d in range(1, FAR + 1):
         for hop in range(1, d + 1):
             for s, p in legs_a(d):
@@ -423,7 +434,13 @@
                 for kind in range(3):
                     plane_copy(half, unit, leg, s, kind).wait_send()
     last_b.wait()
-    for d in range(1, FAR + 1):
+    for d in (2, 4):
+        for s in range(2):
+            zb_copy(s, d, d).wait_recv()
+    for plane, low, value in products(gather(rc)):
+        at = (plane, slice(cut, None), slice(cut, None)) if low else (plane, slice(0, cut))
+        sums[at] += value
+    for d in (1, 3):
         for s in range(2):
             zb_copy(s, d, d).wait_recv()
     for d in range(1, FAR + 1):
@@ -443,7 +460,7 @@
     operands = [
         pltpu.with_memory_space_constraint(a, pltpu.HBM) for a in (voltages, taps, table)
     ]
-    gathered = (ZL, NX, NY, ZH, NC) + block
+    gathered = (NX, NY, ZH, NC) + block
     return pl.pallas_call(
         exchange_kernel,
         name="exchange",
@@ -454,6 +471,7 @@
         in_specs=[pl.BlockSpec(memory_space=pltpu.HBM)] * 3,
         out_specs=(pl.BlockSpec(memory_space=vmem),) * 2,
         scratch_shapes=[
+            vmem((ZL,) + gathered, bf16),
             vmem(gathered, bf16),
             vmem((rows, samples), bf16),
             vmem(taps.shape, taps.dtype),
@@ -473,7 +491,7 @@
             vmem((2, NX, NZ // 2, NC, NY) + block, bf16),
             vmem((2, 2, 2, NZ // 4, NC, NY) + block, bf16),
             vmem((2, 2, 2, NX, NZ // 4, NC) + block, bf16),
-            dma((PIECES + 2,)), dma(()), dma(()), dma((2, 6)),
+            dma((PIECES + 1 + NC,)), dma(()), dma(()), dma((2, 6)),
             pltpu.SemaphoreType.REGULAR((3,)), dma((2,)), dma((2,)),
             dma((2, FAR, FAR, NC)), dma((2, FAR, FAR, NC)),
             dma((2, FAR, FAR)), dma((2, FAR, FAR)),
@@ -497,7 +515,7 @@
         copy.start()
         copies.append(copy)
 
-    for plane, low, value in products(r_ref):
+    for plane, low, value in products([r_ref[t] for t in range(NX)]):
         if low:
             o[plane, cut:, cut:] = (sums[plane, cut:, cut:] + value) * scale
         else:

time: 61.3 us -> 60 us (0.979)
  the two profiles are of different devices: /device:TPU:8 before, /device:TPU:1 now
where the time goes in v6:
time: 60 us; the launch traced here: 59.7 us
  Pallas kernels  59.7 us (100%)
    pallas_call x1, Pallas kernels, exchange(): pl.pallas_call(exchange_kernel, name='exchange', out_shape=(jax.ShapeDtyp...  57.9 us
    pallas_call x1, Pallas kernels, correlate(): pl.pallas_call(functools.partial(correlate_kernel, scale), name='correlat...  1.81 us

profile of v6, /device:TPU:1, one launch (start us, length us, event | category | flops | bytes accessed | tf_op | source)
XLA Modules:
  0.0 59.7 jit_solution(5280800151006724655)
XLA Ops:
  0.0 57.9 %exchange.1 = (bf16[4,4,4,2,16,128]{5,4,3,2,1,0:T(8,128)(2,1)S(1)}, f32[2,512,512]{2,1,0:T(8,128)S(1)}) custom-call(bf16[16,65536]{1,0:T(8,128)(2,1)} %v_hbm.1, f32[4,512]{1,0:T(4,128)} %taps_hbm.1, bf16[512,512]{1,0:T(8,128)(2,1)} %constant.2.clone.table_hbm), custom_call_target="tpu_custom_call" | custom-call | tf_op jit(solution)/shard_map/exchange/pallas_call | solution.py:464
  57.9 1.8 %correlate.1 = f32[1,2,512,512]{3,2,1,0:T(8,128)} custom-call(bf16[4,4,4,2,16,128]{5,4,3,2,1,0:T(8,128)(2,1)S(1)} %get-tuple-element.7.r_ref, f32[2,512,512]{2,1,0:T(8,128)S(1)} %get-tuple-element.8.sums), custom_call_target="tpu_custom_call" | custom-call | tf_op jit(solution)/shard_map/correlate/pallas_call | solution.py:533

commit v7 on v6

--- a/solution.py
+++ b/solution.py
@@ -234,13 +234,15 @@
 
     def za_copy(s, d, hop, part):
         source, target = route(s, d, hop)
-        src = sa.at[part, target] if hop == 1 else ta.at[s, hop - 2, d - 2, part]
+        both = part == NC
+        cores = pl.ds(0, NC) if both else part
+        src = sa.at[cores, target] if hop == 1 else ta.at[s, hop - 2, d - 2, cores]
         dst = (
-            za.at[part, source % ZL * ZH + source // ZL]
+            za.at[cores, source % ZL * ZH + source // ZL]
             if hop == d
-            else ta.at[s, hop - 1, d - 2, part]
-        )
-        at = (s, hop - 1, d - 1, part)
+            else ta.at[s, hop - 1, d - 2, cores]
+        )
+        at = (s, hop - 1, d - 1)
         return remote(src, dst, za_send.at[at], za_recv.at[at], beside[0][s])
 
     def zb_copy(s, d, hop):
@@ -339,8 +341,8 @@
         for unit in range(2):
             own_leg(half, unit, leg).wait()
 
-    def za_forward(hop):
-        for d in range(FAR, hop - 1, -1):
+    def za_forward(hop, high=FAR, low=0):
+        for d in range(high, max(low, hop) - 1, -1):
             for s, p in legs_a(d):
                 za_copy(s, d, hop - 1, p).wait_recv()
                 za_copy(s, d, hop, p).start()
@@ -352,7 +354,7 @@
                 zb_copy(s, d, hop).start()
 
     def legs_a(d):
-        return [(s, part) for part in range(2) for s in range(2) if d < FAR or s == part]
+        return [(s, s if d == FAR else NC) for s in range(2)]
 
     load(middle - 1).wait()
     filter_pieces(middle, PIECES, True)
@@ -360,12 +362,10 @@
     for part in range(NC):
         load_table(part).wait()
         transform(0, part, sa)
-        for s in range(2):
-            if part == 0 and s == 1:
-                pl.semaphore_wait(ready.at[0], 1)
-            for d in range(FAR, 0, -1):
-                if (s, part) in legs_a(d):
-                    za_copy(s, d, 1, part).start()
+    pl.semaphore_wait(ready.at[0], 1)
+    for d in range(FAR, 0, -1):
+        for s, part in legs_a(d):
+            za_copy(s, d, 1, part).start()
     keep_a = pltpu.make_async_copy(sa.at[:, z], za.at[:, zl * ZH + zh], local_sem.at[0, 5])
     keep_a.start()
 
@@ -380,12 +380,14 @@
     core_copy(1, sb).wait()
     own_core(1, sb).wait()
     legs_start(1, 0, first=True)
-    za_forward(2)
+    za_forward(2, FAR, 3)
     legs_forward(1, 0)
+    za_forward(2, 2)
     legs_wait(1, 0)
     legs_start(1, 1)
-    za_forward(3)
+    za_forward(3, FAR, FAR)
     legs_forward(1, 1)
+    za_forward(3, FAR - 1)
     za_forward(4)
     legs_wait(1, 1)
 
@@ -493,7 +495,7 @@
             vmem((2, 2, 2, NX, NZ // 4, NC) + block, bf16),
             dma((PIECES + 1 + NC,)), dma(()), dma(()), dma((2, 6)),
             pltpu.SemaphoreType.REGULAR((3,)), dma((2,)), dma((2,)),
-            dma((2, FAR, FAR, NC)), dma((2, FAR, FAR, NC)),
+            dma((2, FAR, FAR)), dma((2, FAR, FAR)),
             dma((2, FAR, FAR)), dma((2, FAR, FAR)),
             dma((2, 2, 2, 2, 3)), dma((2, 2, 2, 2, 3)),
         ],

time: 60 us -> 60.1 us (level)
  no operation moved by 1% of the time
where the time goes in v7:
time: 60.1 us; the launch traced here: 59.3 us
  Pallas kernels  59.3 us (99%)
    pallas_call x1, Pallas kernels, exchange(): pl.pallas_call(exchange_kernel, name='exchange', out_shape=(jax.ShapeDtyp...  57.5 us
    pallas_call x1, Pallas kernels, correlate(): pl.pallas_call(functools.partial(correlate_kernel, scale), name='correlat...  1.81 us

profile of v7, /device:TPU:1, one launch (start us, length us, event | category | flops | bytes accessed | tf_op | source)
XLA Modules:
  0.0 59.3 jit_solution(890365119259456467)
XLA Ops:
  0.0 57.5 %exchange.1 = (bf16[4,4,4,2,16,128]{5,4,3,2,1,0:T(8,128)(2,1)S(1)}, f32[2,512,512]{2,1,0:T(8,128)S(1)}) custom-call(bf16[16,65536]{1,0:T(8,128)(2,1)} %v_hbm.1, f32[4,512]{1,0:T(4,128)} %taps_hbm.1, bf16[512,512]{1,0:T(8,128)(2,1)} %constant.2.clone.table_hbm), custom_call_target="tpu_custom_call" | custom-call | tf_op jit(solution)/shard_map/exchange/pallas_call | solution.py:466
  57.5 1.8 %correlate.1 = f32[1,2,512,512]{3,2,1,0:T(8,128)} custom-call(bf16[4,4,4,2,16,128]{5,4,3,2,1,0:T(8,128)(2,1)S(1)} %get-tuple-element.7.r_ref, f32[2,512,512]{2,1,0:T(8,128)S(1)} %get-tuple-element.8.sums), custom_call_target="tpu_custom_call" | custom-call | tf_op jit(solution)/shard_map/correlate/pallas_call | solution.py:535
